TPU v7x, 32 devices: a whole 2x2x4 slice. The times are simulated.
32 devices in a mesh: atom: 16 (over z, x, core), energy: 2 (over y).
Axes of the slice: x: 2, y: 2, z: 4, core: 2. Of those that a mesh axis runs over, the one named last changes fastest.
Arguments:
- single_site: float32 [256, 2, 2, 1024], P('atom', 'energy'), may hold values from -2 to 2
- structure: float32 [2, 26, 2, 1024], P('energy'), may hold values from -0.4375 to 0.4375
- neighbours: int32 [256, 26], P('atom'), may hold values from 0 to 255, as said below
- species: int32 [256], P('atom'), may hold values from 0 to 1
- valence: float32 [2], replicated, may hold values from 0.5 to 3
- energy_weights: float32 [2, 2], P('energy'), may hold values from -4 to 4
- gaunt_table: float32 [49, 1024], replicated, may hold values from -1.5 to 1.5
- radial_shapes: float32 [2, 2, 2, 49, 512], P(None, 'energy'), may hold values from -6 to 6
- radial_weights: float32 [512], replicated, may hold values from 0.001 to 0.03
- madelung: float32 [256, 256], P('atom'), may hold values from -0.375 to 0.375
- old_potential: float32 [256, 49, 512], P('atom', None, 'energy'), may hold values from -6 to 6
Outputs:
- density: float32 [256, 49, 512], P('atom', None, 'energy')
- potential: float32 [256, 49, 512], P('atom', None, 'energy')
Inputs may be any that keep to these rules, and one draw needn't show every extreme that they name: `neighbours`: atom a lies in lattice plane a // 16; the 16 planes close periodically. Slots 0 to 8 name distinct atoms of the plane before a's, slots 9 to 16 distinct atoms of a's own plane other than a, slots 17 to 25 distinct atoms of the plane after. Direction 26 - 1 - k is the reverse of direction k; this only says which structure constants pair up, and the neighbour lists need not be reciprocal.
All inputs are finite; a program needn't handle non-finite values.
Results may differ from a plain program's by a relative error of at most 0.0001.
Values sent between devices are 32-bit elements; how exact they have to be, the bound alone decides.
A program may use at most 64 MiB of HBM per device.

v0:
```python
import jax
import jax.numpy as jnp
from jax import lax
from jax.sharding import PartitionSpec as P

ORDER = 32
DIRS = 26
PLANE = 16
TERMS = 4
SPECIES = 2


mixing = 0.3
highest = lax.Precision.HIGHEST


def with_halo(block, sides, width):
    for axis, dim in sides:
        count = lax.axis_size(axis)
        forward = [(i, i + 1) for i in range(count - 1)]
        forward.append((count - 1, 0))
        backward = [(target, source) for source, target in forward]
        low = lax.ppermute(
            lax.slice_in_dim(block, block.shape[dim] - width, None, axis=dim), axis, forward
        )
        high = lax.ppermute(lax.slice_in_dim(block, 0, width, axis=dim), axis, backward)
        block = jnp.concatenate([low, block, high], axis=dim)
    return block


def matmul_high(former, latter):
    return jnp.matmul(former, latter, precision=highest)


def complex_product(former, latter):
    former_real = former[..., 0, :, :]
    former_imag = former[..., 1, :, :]
    latter_real = latter[..., 0, :, :]
    latter_imag = latter[..., 1, :, :]
    real_part = matmul_high(former_real, latter_real) - matmul_high(former_imag, latter_imag)
    imag_part = matmul_high(former_real, latter_imag) + matmul_high(former_imag, latter_real)
    return jnp.stack([real_part, imag_part], axis=-3)


def shards(
    single_site,
    structure,
    neighbours,
    species,
    valence,
    energy_weights,
    gaunt_table,
    radial_shapes,
    radial_weights,
    madelung,
    old_potential,
):
    atom_rows = single_site.shape[0]
    energy_rows = single_site.shape[1]
    extended = with_halo(single_site, (("atom", 0),), PLANE)
    extended = extended.reshape(extended.shape[0], energy_rows, 2, ORDER, ORDER)
    site_matrices = single_site.reshape(atom_rows, energy_rows, 2, ORDER, ORDER)
    couplings = structure.reshape(energy_rows, DIRS, 2, ORDER, ORDER)
    first_atom = lax.axis_index("atom") * atom_rows
    total_atoms = lax.axis_size("atom") * atom_rows
    local_rows = (neighbours - first_atom + PLANE) % total_atoms
    group_size = DIRS // 2
    forward_all = jnp.moveaxis(couplings, 1, 0)
    backward_all = forward_all[::-1]
    forward_groups = forward_all.reshape(2, group_size, energy_rows, 2, ORDER, ORDER)
    backward_groups = backward_all.reshape(2, group_size, energy_rows, 2, ORDER, ORDER)
    row_groups = jnp.transpose(local_rows).reshape(2, group_size, atom_rows)

    def add_group(accumulated, inputs):
        forward, backward, rows = inputs
        gathered = jnp.take(extended, rows, axis=0)
        left = complex_product(forward[:, None], gathered)
        terms = complex_product(left, backward[:, None])
        return (accumulated + jnp.sum(terms, axis=0), None)

    coupled, _ = lax.scan(
        add_group, jnp.zeros_like(site_matrices), (forward_groups, backward_groups, row_groups)
    )
    propagator = complex_product(site_matrices, coupled)
    series_term = site_matrices
    path_operator = site_matrices
    for power in range(TERMS - 1):
        series_term = complex_product(propagator, series_term)
        path_operator = path_operator + series_term
    flat = path_operator.reshape(atom_rows, energy_rows, 2, ORDER * ORDER)
    projected = jnp.einsum("aezq,lq->aezl", flat, gaunt_table, precision=highest)
    weight_real = energy_weights[:, 0][None, :, None]
    weight_imag = energy_weights[:, 1][None, :, None]
    scaled_real = weight_real * projected[:, :, 0] - weight_imag * projected[:, :, 1]
    scaled_imag = weight_real * projected[:, :, 1] + weight_imag * projected[:, :, 0]
    slice_width = old_potential.shape[2]
    energy_index = lax.axis_index("energy")
    kinds = jnp.arange(SPECIES, dtype=jnp.int32)
    one_hot = jnp.where(species[:, None] == kinds[None, :], jnp.float32(1.0), jnp.float32(0.0))
    valence_of = jnp.sum(one_hot * valence[None, :], axis=1)
    pieces = lax.all_to_all(radial_shapes, "energy", split_axis=4, concat_axis=1, tiled=True)
    all_real, all_imag = (
        lax.all_gather(scaled_real, "energy", axis=1, tiled=True),
        lax.all_gather(scaled_imag, "energy", axis=1, tiled=True),
    )
    sorted_real = one_hot[:, :, None, None] * all_real[:, None]
    sorted_imag = one_hot[:, :, None, None] * all_imag[:, None]
    density = jnp.einsum("asel,selr->alr", sorted_real, pieces[:, :, 1], precision=highest)
    density = density + jnp.einsum(
        "asel,selr->alr", sorted_imag, pieces[:, :, 0], precision=highest
    )
    piece_weights = lax.dynamic_slice_in_dim(
        radial_weights, energy_index * slice_width, slice_width
    )
    partial_charge = jnp.dot(density[:, 0, :], piece_weights, precision=highest)
    local_charge = lax.psum(partial_charge, "energy") - valence_of
    charges = lax.all_gather(local_charge, "atom", axis=0, tiled=True)
    madelung_shift = jnp.dot(madelung, charges, precision=highest)
    channel = jnp.arange(density.shape[1], dtype=jnp.int32)[None, :, None]
    added = jnp.where(channel == 0, madelung_shift[:, None, None], jnp.float32(0.0))
    potential = (1.0 - mixing) * old_potential + mixing * (density + added)
    return (density, potential)


def solution(mesh):
    in_specs = (
        P("atom", "energy", None, None),
        P("energy", None, None, None),
        P("atom", None),
        P("atom"),
        P(),
        P("energy", None),
        P(),
        P(None, "energy", None, None, None),
        P(),
        P("atom", None),
        P("atom", None, "energy"),
    )
    out_specs = (P("atom", None, "energy"), P("atom", None, "energy"))
    return jax.shard_map(shards, mesh=mesh, in_specs=in_specs, out_specs=out_specs, check_vma=False)
```

profile of v0, /device:TPU:0, one launch (start us, length us, event | category | flops | bytes accessed | tf_op | source)
XLA Modules:
  0.0 190.3 jit_solution(6027028950451602410)
XLA Ops:
  1.2 5.0 %collective-permute-start.1 = (f32[16,1,2,1024]{3,2,1,0:T(2,128)}, f32[16,1,2,1024]{3,2,1,0:T(2,128)S(1)}, u32[]{:S(2)}, u32[]{:S(2)}) collective-permute-start(f32[16,1,2,1024]{3,2,1,0:T(2,128)} %param.13), channel_id=1, source_target_pairs={{2,0},{4,2},{6,4},{8,6},{10,8},{12,10},{14,12},{16,14},{18,16},{20... | collective-permute-start | bytes 393224 | tf_op jit(solution)/shard_map/ppermute | solution.py:26
  6.3 1.6 copy.132
  7.9 2.5 %reshape.313 = f32[2,1,50176]{2,1,0:T(1,128)} reshape(f32[512,2,1,2,49]{4,3,2,1,0:T(2,128)S(1)} %bitcast.241) | data formatting | bytes 802816
  10.4 4.2 %all-to-all-start = ((f32[2,1,50176]{2,1,0:T(1,128)}), f32[2,1,50176]{2,1,0:T(1,128)}, u32[]{:S(2)}, u32[]{:S(2)}) async-start(f32[2,1,50176]{2,1,0:T(1,128)} %reshape.313), calls=%async_computation | async-start | bytes 802816 | tf_op jit(solution)/shard_map/all_to_all | solution.py:101
  14.6 1.1 multiply_reduce_fusion
  16.7 1.3 reshape_transpose_reshape.3
  18.0 1.0 reshape.276
  19.1 1.1 rev.3
  20.2 0.6 dynamic_slice.14
  20.8 0.7 dynamic-slice
  22.9 0.7 reshape.312
  23.6 100.0 %while.11 = (s32[]{:T(128)}, f32[16,1,2,32,32]{4,3,0,2,1:T(8,128)S(1)}, f32[2,13,1,2,32,32]{5,4,3,1,0,2:T(8,128)}, s32[2,13,16]{1,0,2:T(2,128)S(1)}, f32[48,1,2,...) while((s32[]{:T(128)}, ...), condition=%wide.region_2.3_spmd.clone, body=%wide.region_0.2_spmd.clone.sunk | while | flops 656476992 | bytes 64435708 | solution.py:81
  42.8 3.9 %gather_fusion = f32[208,2,32,32]{3,2,1,0:T(8,128)} fusion(f32[48,2,32,32]{3,2,1,0:T(8,128)S(1)} %bitcast.229, s32[1024]{0:T(1024)S(1)} %pad_clamp_fusion.2), kind=kCustom, calls=%fused_computation.clone.clone.1 | custom fusion | bytes 3408704 | tf_op jit(solution)/shard_map/while/body/eval_jaxpr/jit(_take)/gather | solution.py:76
  46.6 3.7 %copy.172 = f32[208,2,32,32]{3,2,0,1:T(8,128)S(1)} copy(f32[208,2,32,32]{3,2,1,0:T(8,128)} %gather_fusion) | data formatting | bytes 3407872 | tf_op jit(solution)/shard_map/while/body/eval_jaxpr/jit(_take)/gather | solution.py:76
  51.9 3.2 %fusion.81 = f32[13,32,16,32]{3,1,2,0:T(8,128)S(1)} fusion(f32[13,16,1,2,32,32]{5,4,1,0,3,2:T(8,128)S(1)} %broadcast_select_fusion.3, f32[13,1,1,2,32,32]{5,4,0,3,2,1:T(8,128)S(1)} %bitcast.235), kind=kOutput, calls=%fused_computation.16.clone.1 | convolution fusion | flops 81788928 | bytes 4472832 | tf_op jit(solution)/shard_map/while/body/eval_jaxpr/dot_general | solution.py:32
  55.1 3.3 %fusion.82 = f32[13,32,16,32]{3,1,2,0:T(8,128)S(1)} fusion(f32[13,32,16,32]{3,1,2,0:T(8,128)S(1)} %fusion.81, f32[13,16,1,2,32,32]{5,4,1,0,3,2:T(8,128)S(1)} %broadcast_select_fusion.3, f32[13,1,1,2,32,32]{5,4,0,3,2,1:T(8,128)S(1)} %bitcast.236), kind=kOutput, calls=%fused_computation.19.clone.1 | convolution fusion | flops 82001920 | bytes 7880704 | tf_op jit(solution)/shard_map/while/body/eval_jaxpr/dot_general | solution.py:32
  58.4 3.2 %fusion.78 = f32[13,32,16,32]{3,1,2,0:T(8,128)S(1)} fusion(f32[13,16,1,2,32,32]{5,4,1,0,3,2:T(8,128)S(1)} %broadcast_select_fusion.3, f32[13,1,1,2,32,32]{5,4,0,3,2,1:T(8,128)S(1)} %bitcast.237), kind=kOutput, calls=%fused_computation.15.clone.1 | convolution fusion | flops 81788928 | bytes 4472832 | tf_op jit(solution)/shard_map/while/body/eval_jaxpr/dot_general | solution.py:32
  61.6 3.3 %fusion.79 = f32[13,32,16,32]{3,1,2,0:T(8,128)S(1)} fusion(f32[13,32,16,32]{3,1,2,0:T(8,128)S(1)} %fusion.78, f32[13,16,1,2,32,32]{5,4,1,0,3,2:T(8,128)S(1)} %broadcast_select_fusion.3, f32[13,1,1,2,32,32]{5,4,0,3,2,1:T(8,128)S(1)} %bitcast.238), kind=kOutput, calls=%fused_computation.20.clone.1 | convolution fusion | flops 82001920 | bytes 7880704 | tf_op jit(solution)/shard_map/while/body/eval_jaxpr/dot_general | solution.py:32
  64.9 3.3 %fusion.83 = f32[13,16,32,32]{3,2,1,0:T(8,128)S(1)} fusion(f32[13,32,16,32]{3,1,2,0:T(8,128)S(1)} %fusion.79, f32[13,1,1,2,32,32]{5,4,0,3,2,1:T(8,128)S(1)} %bitcast.231), kind=kOutput, calls=%fused_computation.6.clone.1 | convolution fusion | flops 81788928 | bytes 4472832 | tf_op jit(solution)/shard_map/while/body/eval_jaxpr/dot_general | solution.py:32
  68.2 3.4 %subtract_bitcast_fusion.2 = f32[13,16,1,1,32,32]{5,4,1,0,3,2:T(8,128)S(1)} fusion(f32[13,16,32,32]{3,2,1,0:T(8,128)S(1)} %fusion.83, f32[13,32,16,32]{3,1,2,0:T(8,128)S(1)} %fusion.82, f32[13,1,1,2,32,32]{5,4,0,3,2,1:T(8,128)S(1)} %bitcast.232), kind=kOutput, calls=%fused_computation.13.clone.1 | convolution fusion | flops 82001920 | bytes 7880704 | tf_op jit(solution)/shard_map/while/body/eval_jaxpr/dot_general | solution.py:32
  71.6 3.3 %fusion.80 = f32[13,16,32,32]{3,2,1,0:T(8,128)S(1)} fusion(f32[13,32,16,32]{3,1,2,0:T(8,128)S(1)} %fusion.79, f32[13,1,1,2,32,32]{5,4,0,3,2,1:T(8,128)S(1)} %bitcast.233), kind=kOutput, calls=%fused_computation.4.clone.1 | convolution fusion | flops 81788928 | bytes 4472832 | tf_op jit(solution)/shard_map/while/body/eval_jaxpr/dot_general | solution.py:32
  74.9 3.4 %add_bitcast_fusion.2 = f32[13,16,1,1,32,32]{5,4,1,0,3,2:T(8,128)S(1)} fusion(f32[13,16,32,32]{3,2,1,0:T(8,128)S(1)} %fusion.80, f32[13,32,16,32]{3,1,2,0:T(8,128)S(1)} %fusion.82, f32[13,1,1,2,32,32]{5,4,0,3,2,1:T(8,128)S(1)} %bitcast.234), kind=kOutput, calls=%fused_computation.12.clone.1 | convolution fusion | flops 82001920 | bytes 7880704 | tf_op jit(solution)/shard_map/while/body/eval_jaxpr/dot_general | solution.py:32
  78.2 0.9 maximum_reduce_fusion.2
  79.5 3.9 %gather_fusion = f32[208,2,32,32]{3,2,1,0:T(8,128)} fusion(f32[48,2,32,32]{3,2,1,0:T(8,128)S(1)} %bitcast.229, s32[1024]{0:T(1024)S(1)} %pad_clamp_fusion.2), kind=kCustom, calls=%fused_computation.clone.clone.1 | custom fusion | bytes 3408704 | tf_op jit(solution)/shard_map/while/body/eval_jaxpr/jit(_take)/gather | solution.py:76
  83.4 3.7 %copy.172 = f32[208,2,32,32]{3,2,0,1:T(8,128)S(1)} copy(f32[208,2,32,32]{3,2,1,0:T(8,128)} %gather_fusion) | data formatting | bytes 3407872 | tf_op jit(solution)/shard_map/while/body/eval_jaxpr/jit(_take)/gather | solution.py:76
  88.7 3.2 %fusion.81 = f32[13,32,16,32]{3,1,2,0:T(8,128)S(1)} fusion(f32[13,16,1,2,32,32]{5,4,1,0,3,2:T(8,128)S(1)} %broadcast_select_fusion.3, f32[13,1,1,2,32,32]{5,4,0,3,2,1:T(8,128)S(1)} %bitcast.235), kind=kOutput, calls=%fused_computation.16.clone.1 | convolution fusion | flops 81788928 | bytes 4472832 | tf_op jit(solution)/shard_map/while/body/eval_jaxpr/dot_general | solution.py:32
  91.9 3.3 %fusion.82 = f32[13,32,16,32]{3,1,2,0:T(8,128)S(1)} fusion(f32[13,32,16,32]{3,1,2,0:T(8,128)S(1)} %fusion.81, f32[13,16,1,2,32,32]{5,4,1,0,3,2:T(8,128)S(1)} %broadcast_select_fusion.3, f32[13,1,1,2,32,32]{5,4,0,3,2,1:T(8,128)S(1)} %bitcast.236), kind=kOutput, calls=%fused_computation.19.clone.1 | convolution fusion | flops 82001920 | bytes 7880704 | tf_op jit(solution)/shard_map/while/body/eval_jaxpr/dot_general | solution.py:32
  95.2 3.2 %fusion.78 = f32[13,32,16,32]{3,1,2,0:T(8,128)S(1)} fusion(f32[13,16,1,2,32,32]{5,4,1,0,3,2:T(8,128)S(1)} %broadcast_select_fusion.3, f32[13,1,1,2,32,32]{5,4,0,3,2,1:T(8,128)S(1)} %bitcast.237), kind=kOutput, calls=%fused_computation.15.clone.1 | convolution fusion | flops 81788928 | bytes 4472832 | tf_op jit(solution)/shard_map/while/body/eval_jaxpr/dot_general | solution.py:32
  98.4 3.3 %fusion.79 = f32[13,32,16,32]{3,1,2,0:T(8,128)S(1)} fusion(f32[13,32,16,32]{3,1,2,0:T(8,128)S(1)} %fusion.78, f32[13,16,1,2,32,32]{5,4,1,0,3,2:T(8,128)S(1)} %broadcast_select_fusion.3, f32[13,1,1,2,32,32]{5,4,0,3,2,1:T(8,128)S(1)} %bitcast.238), kind=kOutput, calls=%fused_computation.20.clone.1 | convolution fusion | flops 82001920 | bytes 7880704 | tf_op jit(solution)/shard_map/while/body/eval_jaxpr/dot_general | solution.py:32
  101.7 3.3 %fusion.83 = f32[13,16,32,32]{3,2,1,0:T(8,128)S(1)} fusion(f32[13,32,16,32]{3,1,2,0:T(8,128)S(1)} %fusion.79, f32[13,1,1,2,32,32]{5,4,0,3,2,1:T(8,128)S(1)} %bitcast.231), kind=kOutput, calls=%fused_computation.6.clone.1 | convolution fusion | flops 81788928 | bytes 4472832 | tf_op jit(solution)/shard_map/while/body/eval_jaxpr/dot_general | solution.py:32
  105.0 3.4 %subtract_bitcast_fusion.2 = f32[13,16,1,1,32,32]{5,4,1,0,3,2:T(8,128)S(1)} fusion(f32[13,16,32,32]{3,2,1,0:T(8,128)S(1)} %fusion.83, f32[13,32,16,32]{3,1,2,0:T(8,128)S(1)} %fusion.82, f32[13,1,1,2,32,32]{5,4,0,3,2,1:T(8,128)S(1)} %bitcast.232), kind=kOutput, calls=%fused_computation.13.clone.1 | convolution fusion | flops 82001920 | bytes 7880704 | tf_op jit(solution)/shard_map/while/body/eval_jaxpr/dot_general | solution.py:32
  108.3 3.3 %fusion.80 = f32[13,16,32,32]{3,2,1,0:T(8,128)S(1)} fusion(f32[13,32,16,32]{3,1,2,0:T(8,128)S(1)} %fusion.79, f32[13,1,1,2,32,32]{5,4,0,3,2,1:T(8,128)S(1)} %bitcast.233), kind=kOutput, calls=%fused_computation.4.clone.1 | convolution fusion | flops 81788928 | bytes 4472832 | tf_op jit(solution)/shard_map/while/body/eval_jaxpr/dot_general | solution.py:32
  111.6 3.4 %add_bitcast_fusion.2 = f32[13,16,1,1,32,32]{5,4,1,0,3,2:T(8,128)S(1)} fusion(f32[13,16,32,32]{3,2,1,0:T(8,128)S(1)} %fusion.80, f32[13,32,16,32]{3,1,2,0:T(8,128)S(1)} %fusion.82, f32[13,1,1,2,32,32]{5,4,0,3,2,1:T(8,128)S(1)} %bitcast.234), kind=kOutput, calls=%fused_computation.12.clone.1 | convolution fusion | flops 82001920 | bytes 7880704 | tf_op jit(solution)/shard_map/while/body/eval_jaxpr/dot_general | solution.py:32
  115.0 0.9 maximum_reduce_fusion.2
  127.3 0.6 convolution_subtract_fusion.2
  128.5 0.6 convolution_add_fusion.2
  129.7 0.6 convolution_subtract_fusion.1
  132.8 0.6 convolution_subtract_fusion
  134.9 1.2 multiply_subtract_fusion
  136.2 4.4 %all-gather.1 = f32[16,2,1,49]{3,0,2,1:T(8,128)S(1)} all-gather(f32[16,1,1,49]{3,0,2,1:T(8,128)S(1)} %get-tuple-element.89), channel_id=3, replica_groups=mesh['atom'=16,'energy'=2] {'energy'}, dimensions={1}, use_global_device_ids=true | all-gather | bytes 9408 | tf_op jit(solution)/shard_map/all_gather | solution.py:104
  140.6 4.6 %all-gather = f32[16,2,1,49]{3,0,2,1:T(8,128)S(1)} all-gather(f32[16,1,1,49]{3,0,2,1:T(8,128)S(1)} %get-tuple-element.88), channel_id=2, replica_groups=mesh['atom'=16,'energy'=2] {'energy'}, dimensions={1}, use_global_device_ids=true | all-gather | bytes 9408 | tf_op jit(solution)/shard_map/all_gather | solution.py:103
  145.8 2.8 %reduce.1 = f32[2,50176]{1,0:T(2,128)S(1)} reduce(f32[2,1,50176]{2,1,0:T(1,128)} %all-to-all-done, f32[]{:T(128)} %broadcast.157), dimensions={1}, to_apply=%all_to_all.13.reduce_sub_computation | reduce | bytes 802820 | tf_op jit(solution)/shard_map/all_to_all | solution.py:101
  148.6 1.8 reshape.314
  151.0 0.9 convolution_bitcast_fusion
  152.0 1.0 fusion.19
  153.1 4.9 %psum.7 = f32[16]{0:T(128)S(1)} all-reduce(f32[16]{0:T(128)S(1)} %convolution_bitcast_fusion.4), channel_id=1, replica_groups=mesh['atom'=16,'energy'=2] {'energy'}, use_global_device_ids=true, to_apply=%region_3.4 | all-reduce | flops 16 | bytes 128 | tf_op jit(solution)/shard_map/psum | solution.py:116
  158.1 29.5 %all-reduce = f32[256]{0:T(256)S(1)} all-reduce(f32[256]{0:T(256)S(1)} %subtract_dynamic-update-slice_fusion), channel_id=1, replica_groups=mesh['atom'=16,'energy'=2] {'atom'}, use_global_device_ids=true, to_apply=%add | all-reduce | flops 256 | bytes 2048
  187.8 2.2 %multiply_add_fusion = f32[16,49,256]{2,0,1:T(8,128)} fusion(f32[16,49,256]{2,0,1:T(8,128)S(1)} %fusion.19, f32[16,49,256]{2,0,1:T(8,128)} %param.23, f32[16,49]{0,1:T(8,128)S(1)} %broadcast_select_fusion.1), kind=kLoop, calls=%fused_computation.50 | loop fusion | flops 802816 | bytes 2411584 | tf_op jit(solution)/shard_map/add | solution.py:121
  (106 shorter events, 16.6 us)
Async XLA Ops:
  0.6 134.0 %copy-start = (f32[49,1024]{1,0:T(8,128)S(1)}, f32[49,1024]{1,0:T(8,128)}, u32[]{:S(2)}) copy-start(f32[49,1024]{1,0:T(8,128)} %param.19) | copy-start | bytes 602116
  0.6 15.7 %copy-start.5 = (f32[16,1,2,1024]{3,2,1,0:T(2,128)S(1)}, f32[16,1,2,1024]{3,2,1,0:T(2,128)}, u32[]{:S(2)}) copy-start(f32[16,1,2,1024]{3,2,1,0:T(2,128)} %param.13) | copy-start | bytes 393220
  0.7 13.9 %copy-start.10 = (s32[16,26]{1,0:T(8,128)S(1)}, s32[16,26]{1,0:T(8,128)}, u32[]{:S(2)}) copy-start(s32[16,26]{1,0:T(8,128)} %param.15) | copy-start | bytes 4996
  0.7 14.0 %copy-start.15 = (s32[16]{0:T(128)S(1)}, s32[16]{0:T(128)}, u32[]{:S(2)}) copy-start(s32[16]{0:T(128)} %param.16) | copy-start | bytes 196
  0.7 14.0 %copy-start.14 = (f32[2]{0:T(128)S(1)}, f32[2]{0:T(128)}, u32[]{:S(2)}) copy-start(f32[2]{0:T(128)} %param.17) | copy-start | bytes 28
  0.7 15.7 %copy-start.7 = (f32[1,26,2,1024]{3,2,1,0:T(2,128)S(1)}, f32[1,26,2,1024]{3,2,1,0:T(2,128)}, u32[]{:S(2)}) copy-start(f32[1,26,2,1024]{3,2,1,0:T(2,128)} %param.14) | copy-start | bytes 638980
  0.7 22.0 %collective-permute-start = (f32[16,1,2,1024]{3,2,1,0:T(2,128)}, f32[16,1,2,1024]{3,2,1,0:T(2,128)S(1)}, u32[]{:S(2)}, u32[]{:S(2)}) collective-permute-start(f32[16,1,2,1024]{3,2,1,0:T(2,128)} %param.13), channel_id=1, source_target_pairs={{0,2},{2,4},{4,6},{6,8},{8,10},{10,12},{12,14},{14,16},{16,18},{18... | collective-permute-start | bytes 393224 | tf_op jit(solution)/shard_map/ppermute | solution.py:23
  1.2 21.5 %collective-permute-start.1 = (f32[16,1,2,1024]{3,2,1,0:T(2,128)}, f32[16,1,2,1024]{3,2,1,0:T(2,128)S(1)}, u32[]{:S(2)}, u32[]{:S(2)}) collective-permute-start(f32[16,1,2,1024]{3,2,1,0:T(2,128)} %param.13), channel_id=1, source_target_pairs={{2,0},{4,2},{6,4},{8,6},{10,8},{12,10},{14,12},{16,14},{18,16},{20... | collective-permute-start | bytes 393224 | tf_op jit(solution)/shard_map/ppermute | solution.py:26
  7.9 12.3 %copy-start.16 = (f32[512]{0:T(512)S(1)}, f32[512]{0:T(512)}, u32[]{:S(2)}) copy-start(f32[512]{0:T(512)} %param.21) | copy-start | bytes 6148
  7.9 12.9 %copy-start.18 = (u32[32]{0:T(128)S(1)}, u32[32]{0:T(128)}, u32[]{:S(2)}) copy-start(u32[32]{0:T(128)} %constant.72) | copy-start | bytes 388
  7.9 14.2 %copy-start.12 = (f32[1,2]{1,0:T(1,128)S(1)}, f32[1,2]{1,0:T(1,128)}, u32[]{:S(2)}) copy-start(f32[1,2]{1,0:T(1,128)} %param.18) | copy-start | bytes 28
  10.4 134.9 %all-to-all-start = ((f32[2,1,50176]{2,1,0:T(1,128)}), f32[2,1,50176]{2,1,0:T(1,128)}, u32[]{:S(2)}, u32[]{:S(2)}) async-start(f32[2,1,50176]{2,1,0:T(1,128)} %reshape.313), calls=%async_computation | async-start | bytes 802816 | tf_op jit(solution)/shard_map/all_to_all | solution.py:101
  23.6 100.3 %copy-start.1 = (f32[16,1,2,32,32]{4,3,0,2,1:T(8,128)S(1)}, f32[16,1,2,32,32]{4,3,0,2,1:T(8,128)}, u32[]{:S(2)}) copy-start(f32[16,1,2,32,32]{4,3,0,2,1:T(8,128)} %reshape.276) | copy-start | bytes 393220
  50.4 1.2 copy-start.2
  50.4 1.4 copy-start.3
  87.1 1.2 copy-start.2
  87.1 1.4 copy-start.3
  130.3 4.0 %copy-start.6 = (f32[16,1,2,1024]{3,2,1,0:T(2,128)S(1)}, f32[16,1,2,1024]{3,2,1,0:T(2,128)}, u32[]{:S(2)}) copy-start(f32[16,1,2,1024]{3,2,1,0:T(2,128)} %param.13) | copy-start | bytes 393220
  133.4 17.7 %copy-start.9 = (f32[16,2]{0,1:T(2,128)S(1)}, f32[16,2]{0,1:T(2,128)}, u32[]{:S(2)}) copy-start(f32[16,2]{0,1:T(2,128)} %get-tuple-element.91) | copy-start | bytes 388
  136.1 16.8 %copy-start.11 = (f32[256]{0:T(256)S(1)}, f32[256]{0:T(256)}, u32[]{:S(2)}) copy-start(f32[256]{0:T(256)} %dynamic_slice.14) | copy-start | bytes 3076
  140.5 17.5 %copy-start.13 = (f32[16]{0:T(128)S(1)}, f32[16]{0:T(128)}, u32[]{:S(2)}) copy-start(f32[16]{0:T(128)} %get-tuple-element.90) | copy-start | bytes 196
  140.5 47.1 %copy-start.8 = (f32[16,256]{1,0:T(8,128)S(1)}, f32[16,256]{1,0:T(8,128)}, u32[]{:S(2)}) copy-start(f32[16,256]{1,0:T(8,128)} %param.22) | copy-start | bytes 49156
  140.5 47.2 %copy-start.17 = (pred[49]{0:T(512)(128)(4,1)S(1)}, pred[49]{0:T(512)(128)(4,1)}, u32[]{:S(2)}) copy-start(pred[49]{0:T(512)(128)(4,1)} %iota_compare_fusion) | copy-start | bytes 151
  153.0 37.1 %copy-start.4 = (f32[16,49,256]{2,0,1:T(8,128)}, f32[16,49,256]{2,0,1:T(8,128)S(1)}, u32[]{:S(2)}) copy-start(f32[16,49,256]{2,0,1:T(8,128)S(1)} %fusion.19) | copy-start | bytes 2408452
where the time goes:
time: 194 us; the launch traced here: 190 us
  matrix products  64.2 us (33%)
  blocking collectives  43.3 us (22%)
  local copies, waits for them, and re-layouts  32.3 us (17%)
  loops' own time  26.8 us (14%)
  other arithmetic  11.9 us (6%)
  starting transfers between devices  9.73 us (5%)
  between operations  2.05 us (1%)
    dot_general x32, matrix products, matmul_high(): return jnp.matmul(former, latter, precision=highest)  61.7 us
    unnamed x1, blocking collectives  29.5 us
    another operation x1, loops' own time, shards(): lax.scan(add_group, jnp.zeros_like(site_matrices), (forward_groups, backw...  26.8 us
    gather x4, local copies, waits for them, and re-layouts, add_group(): gathered = jnp.take(extended, rows, axis=0)  15.2 us
    unnamed x40, local copies, waits for them, and re-layouts  6.71 us
    ppermute x1, starting transfers between devices, with_halo(): lax.ppermute(lax.slice_in_dim(block, 0, width, axis=dim), axis, backward)  5.02 us
    psum x1, blocking collectives, shards(): local_charge = lax.psum(partial_charge, 'energy') - valence_of  4.92 us
    all_gather x1, blocking collectives, shards(): lax.all_gather(scaled_real, 'energy', axis=1, tiled=True)  4.56 us
  transfers between devices with their start and end apart: 3, of which 0 were waited for; matrix products, arithmetic and copies ran while one was open for 51% of the time, Pallas kernels for 0%

commit v1 on v0

v1 whole, which is shorter than its diff:
```python
import functools

import jax
import jax.numpy as jnp
from jax import lax
from jax.experimental import pallas as pl
from jax.experimental.pallas import tpu as pltpu
from jax.sharding import PartitionSpec as P

PLANE = 16
TERMS = 4
LANES = 128

mixing = 0.3
f32 = jnp.float32
bf16 = jnp.bfloat16


def split(x):
    high = x.astype(bf16)
    return high, (x - high.astype(f32)).astype(bf16)


def tile_masks(rows):
    lane = lax.broadcasted_iota(jnp.int32, (rows, LANES), 1)
    return lane < 64, (lane & 32) == 0


def times_i(x, real_lane):
    return jnp.where(real_lane, -pltpu.roll(x, 96, 1), pltpu.roll(x, 32, 1))


def dot(a, b):
    return jnp.dot(a, b, preferred_element_type=f32)


def prepare_couplings(g_ref, rhs_ref, order, blocks):
    _, real_lane = tile_masks(order)
    for t in range(blocks):
        lanes = pl.ds(t * LANES, LANES)
        g = g_ref[:, lanes]
        high, low = split(jnp.concatenate([g, times_i(g, real_lane)], axis=0))
        rhs_ref[:, lanes] = jnp.concatenate([high, high, low, low], axis=0)


def plane_products(x, lhs_ref, rhs_ref, rhigh_ref, rlow_ref, plane, first, count, order):
    low_lane, _ = tile_masks(order)
    for pair in range(PLANE // 2):
        v = x(pair)
        high = v.astype(bf16).astype(f32)
        low = v - high
        even = jnp.where(low_lane, high, pltpu.roll(low, 64, 1))
        odd = jnp.where(low_lane, pltpu.roll(high, 64, 1), low)
        lhs_ref[pl.ds(pair * 2 * order, 2 * order), :] = jnp.concatenate(
            [even, odd], axis=0
        ).astype(bf16)
    lhs = lhs_ref[...]
    lhs = jnp.concatenate([lhs, lhs], axis=1)
    for t in range(count):
        r = dot(lhs, rhs_ref[:, pl.ds((first + t) * LANES, LANES)])
        high, low = split(r)
        rhigh_ref[plane, t] = high
        rlow_ref[plane, t] = low


def gather(nbr_ref, rhigh_ref, rlow_ref, yhigh_ref, ylow_ref, dirs, firsts, order):
    for b in range(dirs):
        k = dirs - 1 - b
        plane = 0 if k < 9 else (1 if k < 17 else 2)
        t = b // 2
        half = pl.ds((b % 2) * 64, 64)
        for a in range(PLANE):
            n = nbr_ref[a, k]
            rows = pl.ds(pl.multiple_of(n * order, order), order)
            to = (pl.ds(t * order, order), pl.ds(a * LANES + (b % 2) * 64, 64))
            yhigh_ref[to] = rhigh_ref[plane, t - firsts[plane], rows, half]
            ylow_ref[to] = rlow_ref[plane, t - firsts[plane], rows, half]


def block_diagonal(v, low_lane, real_lane):
    turned = times_i(v, real_lane)
    zero = jnp.zeros_like(v)
    return jnp.concatenate(
        [
            jnp.where(low_lane, v, zero),
            jnp.where(low_lane, turned, zero),
            jnp.where(low_lane, zero, v),
            jnp.where(low_lane, zero, turned),
        ],
        axis=0,
    )


def weights_of(v, low_lane, real_lane):
    high, low = split(block_diagonal(v, low_lane, real_lane))
    return jnp.concatenate([high, low], axis=1)


def pair_product(u, weights, order):
    high, low = split(u)
    o = dot(jnp.concatenate([high, low], axis=0), weights)
    return o[:order, :LANES] + o[order:, :LANES] + o[:order, LANES:]


def path_and_project(own, g2_ref, yhigh_ref, ylow_ref, gaunt_ref, v_ref, order):
    low_lane, real_lane = tile_masks(order)
    low2, _ = tile_masks(2 * order)
    gh, gl = split(g2_ref[...])
    rows = gh.shape[0]
    both = jnp.concatenate([gh, gl], axis=0)
    for pair in range(PLANE // 2):
        lanes = pl.ds(pair * 2 * LANES, 2 * LANES)
        d = dot(both, yhigh_ref[:, lanes])
        s = d[:rows] + d[rows:] + dot(gh, ylow_ref[:, lanes])
        half = rows // 2
        e0, o0 = s[:half, :LANES], s[half:, :LANES]
        e1, o1 = s[:half, LANES:], s[half:, LANES:]
        m = jnp.where(low2, e0, o1) + pltpu.roll(jnp.where(low2, e1, o0), 64, 1)
        c = m[:order] + times_i(m[order:], real_lane)
        t = own(pair)
        q = pair_product(c, weights_of(t, low_lane, real_lane), order)
        wq = weights_of(q, low_lane, real_lane)
        v = t
        for _ in range(TERMS - 1):
            v = t + pair_product(v, wq, order)
        v_ref[pl.ds(pair * order, order), :] = v
    pairs = PLANE // 2
    lane = lax.broadcasted_iota(jnp.int32, (pairs, LANES), 1) // 32
    columns = []
    for block in range(order // 4):
        us = [v_ref[pl.ds(4 * block + ii, pairs, stride=order), :] for ii in range(4)]
        pieces = []
        for part in range(4):
            z = us[0] if part == 0 else pltpu.roll(us[0], (-part * 32) % LANES, 1)
            for ii in range(1, 4):
                shift = ((ii - part) * 32) % LANES
                z = jnp.where(lane == ii, us[ii] if shift == 0 else pltpu.roll(us[ii], shift, 1), z)
            pieces.append(z)
        columns.append(jnp.concatenate(pieces, axis=0))
    z = jnp.concatenate(columns, axis=1)
    zh, zl = split(z)
    gh, gl = split(gaunt_ref[...])
    nt = (((1,), (1,)), ((), ()))
    d = lax.dot_general(jnp.concatenate([zh, zl], axis=0), gh, nt, preferred_element_type=f32)
    return d[: 2 * PLANE] + d[2 * PLANE :] + lax.dot_general(zh, gl, nt, preferred_element_type=f32)


def store_scaled(projected, wr, wi, coef_ref):
    pairs = PLANE // 2
    for a2 in range(2):
        re = projected[a2 * 2 * pairs : a2 * 2 * pairs + pairs]
        im = projected[a2 * 2 * pairs + pairs : (a2 + 1) * 2 * pairs]
        coef_ref[0, pl.ds(a2, pairs, stride=2), :] = wr * re - wi * im
        coef_ref[1, pl.ds(a2, pairs, stride=2), :] = wr * im + wi * re


def plan(dirs):
    ends = ((0, 9), (9, 17), (17, dirs))
    firsts = tuple((dirs - stop) // 2 for _, stop in ends)
    counts = tuple((dirs - 1 - start) // 2 - first + 1 for (start, _), first in zip(ends, firsts))
    return firsts, counts


def core(order, dirs, nbr_ref, w_ref, low_ref, own_ref, high_ref, g_ref, g2_ref, gaunt_ref,
         coef_ref, rhs_ref, lhs_ref, rhigh_ref, rlow_ref, yhigh_ref, ylow_ref, v_ref):
    firsts, counts = plan(dirs)
    prepare_couplings(g_ref, rhs_ref, order, dirs // 2)
    for plane, ref in ((1, own_ref), (0, low_ref), (2, high_ref)):
        x = lambda pair, ref=ref: ref[:, pl.ds(pair * LANES, LANES)]
        plane_products(x, lhs_ref, rhs_ref, rhigh_ref, rlow_ref, plane, firsts[plane], counts[plane], order)
    gather(nbr_ref, rhigh_ref, rlow_ref, yhigh_ref, ylow_ref, dirs, firsts, order)
    own = lambda pair: own_ref[:, pl.ds(pair * LANES, LANES)]
    projected = path_and_project(own, g2_ref, yhigh_ref, ylow_ref, gaunt_ref, v_ref, order)
    store_scaled(projected, w_ref[0, 0], w_ref[0, 1], coef_ref)


def core_scratch(order, dirs):
    count = max(plan(dirs)[1])
    depth = dirs // 2 * order
    return [
        pltpu.VMEM((8 * order, dirs * 64), bf16),
        pltpu.VMEM((PLANE * order, LANES), bf16),
        pltpu.VMEM((3, count, PLANE * order, LANES), bf16),
        pltpu.VMEM((3, count, PLANE * order, LANES), bf16),
        pltpu.VMEM((depth, PLANE * LANES), bf16),
        pltpu.VMEM((depth, PLANE * LANES), bf16),
        pltpu.VMEM((PLANE // 2 * order, LANES), f32),
    ]


def density_kernel(species_ref, coef_ref, pieces_ref, shift_ref, old_ref, density_ref, potential_ref):
    kinds, energies = pieces_ref.shape[0], pieces_ref.shape[1]
    channels, atoms, width = density_ref.shape
    kind = jnp.broadcast_to(species_ref[...], (atoms, width))
    for l in range(channels):
        total = None
        for e in range(energies):
            for z in range(2):
                row = jnp.broadcast_to(pieces_ref[0, e, 1 - z, l : l + 1, :], (atoms, width))
                for s in range(1, kinds):
                    row = jnp.where(kind == s, pieces_ref[s, e, 1 - z, l : l + 1, :], row)
                term = coef_ref[e, z, :, l : l + 1] * row
                total = term if total is None else total + term
        density_ref[l] = total
        added = total + shift_ref[...] if l == 0 else total
        potential_ref[l] = (1.0 - mixing) * old_ref[l] + mixing * added


VMEM = pl.BlockSpec(memory_space=pltpu.VMEM)
SMEM = pl.BlockSpec(memory_space=pltpu.SMEM)


def neighbour_rings(count):
    forward = [(i, (i + 1) % count) for i in range(count)]
    return forward, [(target, source) for source, target in forward]


def shards(single_site, structure, neighbours, species, valence, energy_weights, gaunt_table,
           radial_shapes, radial_weights, madelung, old_potential):
    atom_rows, energy_rows = single_site.shape[:2]
    dirs = structure.shape[1]
    order = int(round(single_site.shape[3] ** 0.5))
    channels, width = old_potential.shape[1], old_potential.shape[2]
    kinds = radial_shapes.shape[0]
    energies = lax.axis_size("energy")
    assert atom_rows == PLANE and energy_rows == 1 and order == 32

    own = single_site.reshape(atom_rows, 2, order, order)
    own = jnp.transpose(own, (2, 0, 1, 3)).reshape(order, atom_rows * 2 * order)
    forward, backward = neighbour_rings(lax.axis_size("atom"))
    low = lax.ppermute(own, "atom", forward)
    high = lax.ppermute(own, "atom", backward)
    pieces = lax.all_to_all(radial_shapes, "energy", split_axis=4, concat_axis=1, tiled=True)

    g = structure.reshape(dirs, 2, order, order)
    g_rows = jnp.transpose(g, (2, 0, 1, 3)).reshape(order, dirs * 2 * order)
    g2 = g[::-1].reshape(dirs // 2, 2, 2, order, order)
    g2 = jnp.transpose(g2, (1, 2, 3, 0, 4)).reshape(4 * order, dirs // 2 * order)

    coef = pl.pallas_call(
        functools.partial(core, order, dirs),
        out_shape=jax.ShapeDtypeStruct((2, atom_rows, channels), f32),
        in_specs=[SMEM, SMEM] + [VMEM] * 6,
        out_specs=VMEM,
        scratch_shapes=core_scratch(order, dirs),
        name="scatter",
    )(neighbours % PLANE, energy_weights, low, own, high, g_rows, g2, gaunt_table)

    shape_charge = jnp.sum(radial_shapes[:, 0, :, 0, :] * radial_weights, axis=-1)
    sums = shape_charge[species]
    part = coef[0, :, 0] * sums[:, 1] + coef[1, :, 0] * sums[:, 0]
    local = lax.psum(part, "energy") - valence[species]
    charges = lax.all_gather(local, "atom", axis=0, tiled=True)
    shift = jnp.sum(madelung * charges[None, :], axis=1, keepdims=True)
    coef_all = lax.all_gather(coef, "energy", axis=0)

    old = jnp.transpose(old_potential, (1, 0, 2))
    density, potential = pl.pallas_call(
        density_kernel,
        out_shape=[jax.ShapeDtypeStruct(old.shape, f32)] * 2,
        in_specs=[VMEM] * 5,
        out_specs=[VMEM] * 2,
        name="density",
    )(species[:, None], coef_all, pieces, shift, old)
    back = lambda x: jnp.transpose(x, (1, 0, 2))
    return back(density), back(potential)


def solution(mesh):
    in_specs = (
        P("atom", "energy", None, None),
        P("energy", None, None, None),
        P("atom", None),
        P("atom"),
        P(),
        P("energy", None),
        P(),
        P(None, "energy", None, None, None),
        P(),
        P("atom", None),
        P("atom", None, "energy"),
    )
    out_specs = (P("atom", None, "energy"), P("atom", None, "energy"))
    return jax.shard_map(shards, mesh=mesh, in_specs=in_specs, out_specs=out_specs, check_vma=False)
```

time: 194 us -> 88 us (0.45); the launches traced: 190 us -> 87.5 us
  matrix products: 64.2 us -> 0 us
  loops' own time: 26.8 us -> 0 us
  Pallas kernels: 0 us -> 12.9 us
  local copies, waits for them, and re-layouts: 32.3 us -> 20.8 us
  other arithmetic: 11.9 us -> 4.07 us
  blocking collectives: 43.3 us -> 39.1 us
    dot_general x37 -> x0, matrix products: 64.2 us -> none  [the longest x32 61.7 us: matmul_high(): return jnp.matmul(former, latter, precision=highest)]
    another operation x1 -> x0, loops' own time: 26.8 us -> none  [shards(): lax.scan(add_group, jnp.zeros_like(site_matrices), (forward_groups, backw...]
    gather x4 -> x2, local copies, waits for them, and re-layouts: 15.2 us -> 1.2 us  [the longest x1 0.64 us: shards(): local = lax.psum(part, 'energy') - valence[species]]
    pallas_call x0 -> x2, Pallas kernels: none -> 12.9 us  [the longest x1 9.89 us: shards(): pl.pallas_call(functools.partial(core, order, dirs), out_shape=jax.ShapeD...]
    all_gather x2 -> x1, blocking collectives: 8.92 us -> 4.68 us  [shards(): coef_all = lax.all_gather(coef, 'energy', axis=0)]
    reshape x3 -> x7, local copies, waits for them, and re-layouts: 1.73 us -> 5.53 us  [the longest x2 1.55 us: shards(): own = single_site.reshape(atom_rows, 2, order, order)]
    add x4 -> x1, other arithmetic: 2.94 us -> 0.01 us  [shards(): part = coef[0, :, 0] * sums[:, 1] + coef[1, :, 0] * sums[:, 0]]
    reduce_sum x3 -> x2, other arithmetic: 2.91 us -> 0.2 us  [the longest x1 0.11 us: shards(): shift = jnp.sum(madelung * charges[None, :], axis=1, keepdims=True)]
  transfers between devices with their start and end apart: 3 -> 3, of which waited for: 0 -> 0; matrix products, arithmetic and copies ran while one was open for 51% -> 16% of each run, Pallas kernels for 0% -> 11%
where the time goes in v1:
time: 88 us; the launch traced here: 87.5 us
  blocking collectives  39.1 us (44%)
  local copies, waits for them, and re-layouts  20.8 us (24%)
  Pallas kernels  12.9 us (15%)
  starting transfers between devices  9.16 us (10%)
  other arithmetic  4.07 us (5%)
  between operations  1.45 us (2%)
    unnamed x1, blocking collectives  29.5 us
    pallas_call x1, Pallas kernels, shards(): pl.pallas_call(functools.partial(core, order, dirs), out_shape=jax.ShapeD...  9.89 us
    unnamed x29, local copies, waits for them, and re-layouts  8.99 us
    ppermute x1, starting transfers between devices, shards(): high = lax.ppermute(own, 'atom', backward)  5.02 us
    psum x1, blocking collectives, shards(): local = lax.psum(part, 'energy') - valence[species]  4.93 us
    all_gather x1, blocking collectives, shards(): coef_all = lax.all_gather(coef, 'energy', axis=0)  4.68 us
    all_to_all x1, starting transfers between devices, shards(): lax.all_to_all(radial_shapes, 'energy', split_axis=4, concat_axis=1, tile...  3.6 us
    pallas_call x1, Pallas kernels, shards(): pl.pallas_call(density_kernel, out_shape=[jax.ShapeDtypeStruct(old.shape,...  3.05 us
  transfers between devices with their start and end apart: 3, of which 0 were waited for; matrix products, arithmetic and copies ran while one was open for 16% of the time, Pallas kernels for 11%

profile of v1, /device:TPU:0, one launch (start us, length us, event | category | flops | bytes accessed | tf_op | source)
XLA Modules:
  0.0 87.5 jit_solution(6365933190174210455)
XLA Ops:
  0.6 1.1 %reshape.24 = f32[16,2,32,32]{3,2,1,0:T(8,128)S(1)} reshape(f32[16,1,2,1024]{3,2,1,0:T(2,128)} %param.11) | data formatting | bytes 262144 | tf_op jit(solution)/shard_map/reshape | solution.py:228
  1.8 0.4 copy.47
  2.2 0.0 copy-start.1
  2.2 0.7 reshape.25.own_ref
  2.9 0.0 copy-start
  2.9 0.5 collective-permute-start
  3.4 5.0 %collective-permute-start.1 = (f32[32,1024]{1,0:T(8,128)S(1)}, f32[32,1024]{1,0:T(8,128)S(1)}, u32[]{:S(2)}, u32[]{:S(2)}) collective-permute-start(f32[32,1024]{1,0:T(8,128)S(1)} %reshape.25.own_ref), channel_id=1, source_target_pairs={{2,0},{4,2},{6,4},{8,6},{10,8},{12,10},{14,12},{16,14},{18,16},{20... | collective-permute-start | bytes 393224 | tf_op jit(solution)/shard_map/ppermute | solution.py:232
  8.5 0.8 copy.37
  9.2 2.5 %reshape.60 = f32[2,1,50176]{2,1,0:T(1,128)} reshape(f32[512,2,1,2,49]{4,3,2,1,0:T(2,128)S(1)} %bitcast.28) | data formatting | bytes 802816
  11.8 3.6 %all-to-all-start = ((f32[2,1,50176]{2,1,0:T(1,128)}), f32[2,1,50176]{2,1,0:T(1,128)S(1)}, u32[]{:S(2)}, u32[]{:S(2)}) async-start(f32[2,1,50176]{2,1,0:T(1,128)} %reshape.60), calls=%async_computation | async-start | bytes 802816 | tf_op jit(solution)/shard_map/all_to_all | solution.py:233
  15.4 0.0 copy-done.7
  15.4 0.0 copy-start.10
  15.4 0.6 add_select_fusion.nbr_ref
  16.0 0.1 copy-done.10
  16.1 0.1 fusion.1
  16.2 0.6 copy-done.9
  16.7 0.6 copy-done.8
  17.4 0.6 fusion.4
  18.0 0.7 copy.40.species_ref
  18.7 0.0 copy-done.2
  18.7 0.4 reshape.26
  19.1 0.1 rev.3
  19.2 0.7 copy.34
  19.8 1.4 %reshape.27.g_ref = f32[32,1664]{1,0:T(8,128)} reshape(f32[32,26,2,32]{3,2,1,0:T(2,128)S(1)} %copy.34) | data formatting | bytes 425984 | tf_op jit(solution)/shard_map/reshape | solution.py:236
  21.2 0.5 copy.42
  21.7 1.0 %reshape.55.g2_ref = f32[128,416]{1,0:T(8,128)} reshape(f32[2,2,32,13,32]{4,3,2,1,0:T(8,128)S(1)} %copy.42) | data formatting | bytes 425984 | tf_op jit(solution)/shard_map/reshape | solution.py:238
  22.8 0.7 copy-done.11
  23.4 0.6 dynamic-slice
  24.7 0.6 gather_fusion
  25.2 0.2 slice_reduce_fusion.2
  25.4 0.0 collective-permute-done.low_ref
  25.4 0.0 collective-permute-done.1.high_ref
  25.4 0.6 copy-done.4
  26.1 0.7 copy-done.5
  26.7 9.9 %scatter.1 = f32[2,16,49]{2,1,0:T(8,128)} custom-call(s32[16,26]{1,0:T(8,128)} %add_select_fusion.nbr_ref, f32[1,2]{1,0:T(1,128)} %w_ref.1, f32[32,1024]{1,0:T(8,128)} %copy-done.4, f32[32,1024]{1,0:T(8,128)} %copy-done, f32[32,1024]{1,0:T(8,128)} %copy-done.5, f32[32,1664]{1,0:T(8,128)} %reshape.27.g_ref, f32[128,416]{1,0:T(8,128)} %reshape.55.g2_ref, ...), custom_call_target="tpu_custom_call" | custom-call | tf_op jit(solution)/shard_map/scatter/pallas_call | solution.py:240
  36.6 0.8 slice_reduce_fusion.3
  37.5 4.9 %psum.7 = f32[16]{0:T(128)S(1)} all-reduce(f32[16]{0:T(128)S(1)} %multiply_add_fusion), channel_id=1, replica_groups=mesh['atom'=16,'energy'=2] {'energy'}, use_global_device_ids=true, to_apply=%region_1.2 | all-reduce | flops 16 | bytes 128 | tf_op jit(solution)/shard_map/psum | solution.py:252
  42.4 1.4 %fusion.3 = f32[256]{0:T(256)S(1)} fusion(f32[256]{0:T(256)S(1)} %broadcast.22, u32[]{:T(128)} %bitcast.12, f32[16]{0:T(128)S(1)} %psum.7, f32[]{:T(128)} %bitcast.10, f32[]{:T(128)} %bitcast.11, s32[16]{0:T(128)S(1)} %copy-done.9), kind=kLoop, calls=%fused_computation.17 | loop fusion | flops 96 | bytes 1548
  43.8 29.5 %all-reduce = f32[256]{0:T(256)S(1)} all-reduce(f32[256]{0:T(256)S(1)} %fusion.3), channel_id=1, replica_groups=mesh['atom'=16,'energy'=2] {'atom'}, use_global_device_ids=true, to_apply=%add | all-reduce | flops 256 | bytes 2048
  73.2 0.1 multiply_reduce_fusion
  73.3 0.7 copy.41.shift_ref
  74.0 4.7 %all-gather = f32[4,16,49]{2,1,0:T(8,128)} all-gather(f32[2,16,49]{2,1,0:T(8,128)S(1)} %copy-done.3), channel_id=2, replica_groups=mesh['atom'=16,'energy'=2] {'energy'}, dimensions={0}, use_global_device_ids=true | all-gather | bytes 18816 | tf_op jit(solution)/shard_map/all_gather | solution.py:255
  78.7 0.0 all-to-all-done
  78.7 0.5 broadcast.41
  79.2 1.9 %reduce.8 = f32[2,50176]{1,0:T(2,128)S(1)} reduce(f32[2,1,50176]{2,1,0:T(1,128)S(1)} %all-to-all-done, f32[]{:T(128)} %broadcast.41), dimensions={1}, to_apply=%all_to_all.13.reduce_sub_computation | reduce | bytes 802820 | tf_op jit(solution)/shard_map/all_to_all | solution.py:233
  81.1 1.8 %reshape.61 = f32[512,2,1,2,49]{4,3,2,1,0:T(2,128)S(1)} reshape(f32[2,50176]{1,0:T(2,128)S(1)} %reduce.8) | data formatting | bytes 802816
  83.0 1.5 %copy.39 = f32[2,1,2,49,2,256]{5,3,2,4,0,1:T(8,128)} copy(f32[2,1,2,49,2,256]{3,2,0,5,4,1:T(2,128)S(1)} %bitcast.27) | data formatting | bytes 802816 | tf_op jit(solution)/shard_map/all_to_all | solution.py:233
  84.5 3.0 %density.1 = (f32[49,16,256]{2,1,0:T(8,128)}, f32[49,16,256]{2,1,0:T(8,128)}) custom-call(s32[16,1]{1,0:T(8,128)} %copy.40.species_ref, f32[2,2,16,49]{3,2,1,0:T(8,128)} %bitcast.33, f32[2,2,2,49,256]{4,3,2,1,0:T(8,128)} %bitcast.31, f32[16,1]{1,0:T(8,128)} %copy.41.shift_ref, f32[49,16,256]{2,1,0:T(8,128)} %bitcast.32), custom_call_target="tpu_custom_call" | custom-call | tf_op jit(solution)/shard_map/density/pallas_call | solution.py:258
  (17 shorter events, 0.0 us)
Async XLA Ops:
  2.2 6.3 %copy-start.1 = (f32[2,1,2,49,512]{4,2,3,1,0:T(2,128)S(1)}, f32[2,1,2,49,512]{4,2,3,1,0:T(2,128)}, u32[]{:S(2)}) copy-start(f32[2,1,2,49,512]{4,2,3,1,0:T(2,128)} %param.18) | copy-start | bytes 1204228
  2.9 6.3 %copy-start = (f32[32,1024]{1,0:T(8,128)}, f32[32,1024]{1,0:T(8,128)S(1)}, u32[]{:S(2)}) copy-start(f32[32,1024]{1,0:T(8,128)S(1)} %reshape.25.own_ref) | copy-start | bytes 393220
  2.9 22.5 %collective-permute-start = (f32[32,1024]{1,0:T(8,128)S(1)}, f32[32,1024]{1,0:T(8,128)S(1)}, u32[]{:S(2)}, u32[]{:S(2)}) collective-permute-start(f32[32,1024]{1,0:T(8,128)S(1)} %reshape.25.own_ref), channel_id=1, source_target_pairs={{0,2},{2,4},{4,6},{6,8},{8,10},{10,12},{12,14},{14,16},{16,18},{18... | collective-permute-start | bytes 393224 | tf_op jit(solution)/shard_map/ppermute | solution.py:231
  3.4 22.0 %collective-permute-start.1 = (f32[32,1024]{1,0:T(8,128)S(1)}, f32[32,1024]{1,0:T(8,128)S(1)}, u32[]{:S(2)}, u32[]{:S(2)}) collective-permute-start(f32[32,1024]{1,0:T(8,128)S(1)} %reshape.25.own_ref), channel_id=1, source_target_pairs={{2,0},{4,2},{6,4},{8,6},{10,8},{12,10},{14,12},{16,14},{18,16},{20... | collective-permute-start | bytes 393224 | tf_op jit(solution)/shard_map/ppermute | solution.py:232
  11.8 3.6 %copy-start.7 = (s32[16,26]{1,0:T(8,128)S(1)}, s32[16,26]{1,0:T(8,128)}, u32[]{:S(2)}) copy-start(s32[16,26]{1,0:T(8,128)} %param.13) | copy-start | bytes 4996
  11.8 6.9 %copy-start.2 = (f32[1,26,2,1024]{3,2,1,0:T(2,128)S(1)}, f32[1,26,2,1024]{3,2,1,0:T(2,128)}, u32[]{:S(2)}) copy-start(f32[1,26,2,1024]{3,2,1,0:T(2,128)} %param.12) | copy-start | bytes 638980
  11.8 67.0 %all-to-all-start = ((f32[2,1,50176]{2,1,0:T(1,128)}), f32[2,1,50176]{2,1,0:T(1,128)S(1)}, u32[]{:S(2)}, u32[]{:S(2)}) async-start(f32[2,1,50176]{2,1,0:T(1,128)} %reshape.60), calls=%async_computation | async-start | bytes 802816 | tf_op jit(solution)/shard_map/all_to_all | solution.py:233
  15.4 0.7 copy-start.10
  16.1 0.7 copy-start.9
  16.7 0.7 copy-start.8
  22.8 0.7 copy-start.11
  25.4 0.7 copy-start.4
  26.1 0.7 copy-start.5
  37.5 35.8 %copy-start.6 = (f32[16,256]{1,0:T(8,128)S(1)}, f32[16,256]{1,0:T(8,128)}, u32[]{:S(2)}) copy-start(f32[16,256]{1,0:T(8,128)} %param.20) | copy-start | bytes 49156
  42.4 31.6 %copy-start.3 = (f32[2,16,49]{2,1,0:T(8,128)S(1)}, f32[2,16,49]{2,1,0:T(8,128)}, u32[]{:S(2)}) copy-start(f32[2,16,49]{2,1,0:T(8,128)} %scatter.1) | copy-start | bytes 18820

commit v2 on v1

--- a/solution.py
+++ b/solution.py
@@ -34,13 +34,46 @@
     return jnp.dot(a, b, preferred_element_type=f32)
 
 
-def prepare_couplings(g_ref, rhs_ref, order, blocks):
+def to_rows(raw, tiles, w_ref, order):
+    stride = w_ref.shape[0] // order
+    lane = lax.broadcasted_iota(jnp.int32, (tiles, LANES), 1) // 32
+    for block in range(order // 4):
+        parts = [raw(m, pl.ds(block * LANES, LANES)) for m in range(4)]
+        for ii in range(4):
+            u = None
+            for m in range(4):
+                shift = ((m - ii) * 32) % LANES
+                x = parts[m] if shift == 0 else pltpu.roll(parts[m], shift, 1)
+                u = x if u is None else jnp.where(lane == m, x, u)
+            w_ref[pl.ds((4 * block + ii) * stride, tiles), :] = u
+
+
+def tile_of(w_ref, tile, order):
+    return w_ref[pl.ds(tile, order, stride=w_ref.shape[0] // order), :]
+
+
+def prepare_couplings(w_ref, rhs_ref, g2_ref, order, blocks):
     _, real_lane = tile_masks(order)
+    lane = lax.broadcasted_iota(jnp.int32, (order, LANES), 1) // 32
+    joined = [None] * 4
     for t in range(blocks):
-        lanes = pl.ds(t * LANES, LANES)
-        g = g_ref[:, lanes]
+        g = tile_of(w_ref, t, order)
         high, low = split(jnp.concatenate([g, times_i(g, real_lane)], axis=0))
-        rhs_ref[:, lanes] = jnp.concatenate([high, high, low, low], axis=0)
+        rhs_ref[:, pl.ds(t * LANES, LANES)] = jnp.concatenate([high, high, low, low], axis=0)
+    for t in range(blocks):
+        g = tile_of(w_ref, blocks - 1 - t, order)
+        place = t % 4
+        for parity in range(2):
+            for z in range(2):
+                row = parity * 2 + z
+                chunk = (2 - 2 * parity + z) % 4
+                shift = ((place - chunk) * 32) % LANES
+                x = g if shift == 0 else pltpu.roll(g, shift, 1)
+                joined[row] = x if place == 0 else jnp.where(lane == place, x, joined[row])
+                if place == 3 or t == blocks - 1:
+                    g2_ref[pl.ds(row * order, order), pl.ds(t // 4 * LANES, 32 * (place + 1))] = (
+                        joined[row][:, : 32 * (place + 1)]
+                    )
 
 
 def plane_products(x, lhs_ref, rhs_ref, rhigh_ref, rlow_ref, plane, first, count, order):
@@ -59,22 +92,21 @@
     for t in range(count):
         r = dot(lhs, rhs_ref[:, pl.ds((first + t) * LANES, LANES)])
         high, low = split(r)
-        rhigh_ref[plane, t] = high
-        rlow_ref[plane, t] = low
-
-
-def gather(nbr_ref, rhigh_ref, rlow_ref, yhigh_ref, ylow_ref, dirs, firsts, order):
-    for b in range(dirs):
-        k = dirs - 1 - b
-        plane = 0 if k < 9 else (1 if k < 17 else 2)
+        rhigh_ref[plane, t] = high.reshape(PLANE, order, LANES)
+        rlow_ref[plane, t] = low.reshape(PLANE, order, LANES)
+
+
+def gather(nbr_ref, rhigh_ref, rlow_ref, yhigh_ref, ylow_ref, dirs, plane, first, order):
+    start, stop = ends_of(dirs)[plane]
+    for k in range(start, stop):
+        b = dirs - 1 - k
         t = b // 2
-        half = pl.ds((b % 2) * 64, 64)
+        half = slice((b % 2) * 64, (b % 2) * 64 + 64)
         for a in range(PLANE):
             n = nbr_ref[a, k]
-            rows = pl.ds(pl.multiple_of(n * order, order), order)
             to = (pl.ds(t * order, order), pl.ds(a * LANES + (b % 2) * 64, 64))
-            yhigh_ref[to] = rhigh_ref[plane, t - firsts[plane], rows, half]
-            ylow_ref[to] = rlow_ref[plane, t - firsts[plane], rows, half]
+            yhigh_ref[to] = rhigh_ref[plane, t - first, n][:, half]
+            ylow_ref[to] = rlow_ref[plane, t - first, n][:, half]
 
 
 def block_diagonal(v, low_lane, real_lane):
@@ -154,51 +186,172 @@
         coef_ref[1, pl.ds(a2, pairs, stride=2), :] = wr * im + wi * re
 
 
+def ends_of(dirs):
+    return ((0, 9), (9, 17), (17, dirs))
+
+
 def plan(dirs):
-    ends = ((0, 9), (9, 17), (17, dirs))
+    ends = ends_of(dirs)
     firsts = tuple((dirs - stop) // 2 for _, stop in ends)
     counts = tuple((dirs - 1 - start) // 2 - first + 1 for (start, _), first in zip(ends, firsts))
     return firsts, counts
 
 
-def core(order, dirs, nbr_ref, w_ref, low_ref, own_ref, high_ref, g_ref, g2_ref, gaunt_ref,
-         coef_ref, rhs_ref, lhs_ref, rhigh_ref, rlow_ref, yhigh_ref, ylow_ref, v_ref):
+def core(order, dirs, ring, energies, nbr_ref, w_ref, valence_ref, own_ref, g_ref, gaunt_ref, shapes_ref,
+         weights_ref, species_ref, madelung_ref, coef_ref, pieces_ref, shift_ref,
+         halo_ref, q_ref, mine_ref, wg_ref, wt_ref, rhs_ref, g2_ref, lhs_ref, rhigh_ref, rlow_ref,
+         yhigh_ref, ylow_ref, v_ref, halo_send, halo_recv, piece_send, piece_recv, coef_send, coef_recv,
+         q_send, q_recv, local_sem):
+    atom, energy = lax.axis_index("atom"), lax.axis_index("energy")
+    devices = ring * energies
+    me = atom * energies + energy
+    kinds, width = shapes_ref.shape[0], pieces_ref.shape[4]
+
+    def place(step):
+        other = lax.rem(me + step, devices)
+        return {"atom": other // energies, "energy": lax.rem(other, energies)}
+
+    barrier = pltpu.get_barrier_semaphore()
+
+    def greet(step, carry):
+        pl.semaphore_signal(barrier, inc=1, device_id=place(step), device_id_type=MESH)
+        return carry
+
+    lax.fori_loop(1, devices, greet, 0)
+
     firsts, counts = plan(dirs)
-    prepare_couplings(g_ref, rhs_ref, order, dirs // 2)
-    for plane, ref in ((1, own_ref), (0, low_ref), (2, high_ref)):
-        x = lambda pair, ref=ref: ref[:, pl.ds(pair * LANES, LANES)]
-        plane_products(x, lhs_ref, rhs_ref, rhigh_ref, rlow_ref, plane, firsts[plane], counts[plane], order)
-    gather(nbr_ref, rhigh_ref, rlow_ref, yhigh_ref, ylow_ref, dirs, firsts, order)
-    own = lambda pair: own_ref[:, pl.ds(pair * LANES, LANES)]
+    to_rows(lambda m, lanes: g_ref[m, :, lanes], dirs // 2, wg_ref, order)
+    prepare_couplings(wg_ref, rhs_ref, g2_ref, order, dirs // 2)
+    pl.semaphore_wait(barrier, devices - 1)
+
+    right, left = lax.rem(atom + 1, ring), lax.rem(atom + ring - 1, ring)
+    halos = []
+    for side, target in ((0, right), (1, left)):
+        copy = pltpu.make_async_remote_copy(
+            src_ref=own_ref, dst_ref=halo_ref.at[side], send_sem=halo_send.at[side],
+            recv_sem=halo_recv.at[side], device_id={"atom": target, "energy": energy}, device_id_type=MESH,
+        )
+        copy.start()
+        halos.append(copy)
+
+    def slice_of(e):
+        return shapes_ref.at[:, :, :, pl.ds(pl.multiple_of(e * width, LANES), width)]
+
+    pieces = []
+    for step in range(1, energies):
+        other = lax.rem(energy + step, energies)
+        copy = pltpu.make_async_remote_copy(
+            src_ref=slice_of(other), dst_ref=pieces_ref.at[energy], send_sem=piece_send.at[step],
+            recv_sem=piece_recv.at[step], device_id={"atom": atom, "energy": other}, device_id_type=MESH,
+        )
+        copy.start()
+        pieces.append(copy)
+    keep = pltpu.make_async_copy(slice_of(energy), pieces_ref.at[energy], local_sem)
+    keep.start()
+
+    def plane(index, raw):
+        w = wt_ref.at[index]
+        to_rows(raw, PLANE // 2, w, order)
+        plane_products(lambda pair: tile_of(w, pair, order), lhs_ref, rhs_ref, rhigh_ref, rlow_ref,
+                       index, firsts[index], counts[index], order)
+        gather(nbr_ref, rhigh_ref, rlow_ref, yhigh_ref, ylow_ref, dirs, index, firsts[index], order)
+
+    plane(1, lambda m, lanes: own_ref[m, :, lanes])
+
+    kind = species_ref[...]
+    sums = [None, None]
+    base = jnp.zeros(kind.shape, f32)
+    for s in range(kinds):
+        total = jnp.sum(shapes_ref[s, 0] * weights_ref[...], axis=1, keepdims=True)
+        for z in range(2):
+            value = jnp.broadcast_to(total[1 - z : 2 - z], kind.shape)
+            sums[z] = value if s == 0 else jnp.where(kind == s, value, sums[z])
+        base = jnp.where(kind == s, valence_ref[s], base)
+    base = jnp.where(energy == 0, base, jnp.zeros_like(base))
+
+    for side, index in ((0, 0), (1, 2)):
+        halos[side].wait_recv()
+        plane(index, lambda m, lanes, side=side: halo_ref[side, m, :, lanes])
+
+    own = lambda pair: tile_of(wt_ref.at[1], pair, order)
     projected = path_and_project(own, g2_ref, yhigh_ref, ylow_ref, gaunt_ref, v_ref, order)
-    store_scaled(projected, w_ref[0, 0], w_ref[0, 1], coef_ref)
-
-
-def core_scratch(order, dirs):
+    store_scaled(projected, w_ref[0, 0], w_ref[0, 1], mine_ref)
+
+    q = mine_ref[0, :, 0:1] * sums[0] + mine_ref[1, :, 0:1] * sums[1] - base
+    row = lax.broadcasted_iota(jnp.int32, (PLANE, LANES), 0)
+    lane = lax.broadcasted_iota(jnp.int32, (PLANE, LANES), 1)
+    spot = lane == row + PLANE * lax.rem(atom, LANES // PLANE)
+    q_ref[me] = jnp.sum(jnp.where(spot, q, jnp.zeros((PLANE, LANES), f32)), axis=0, keepdims=True)
+
+    def spread(step, carry):
+        pltpu.make_async_remote_copy(
+            src_ref=q_ref.at[me], dst_ref=q_ref.at[me], send_sem=q_send, recv_sem=q_recv,
+            device_id=place(step), device_id_type=MESH,
+        ).start()
+        return carry
+
+    lax.fori_loop(1, devices, spread, 0)
+    coefs = []
+    for step in range(1, energies):
+        other = lax.rem(energy + step, energies)
+        copy = pltpu.make_async_remote_copy(
+            src_ref=mine_ref, dst_ref=coef_ref.at[energy], send_sem=coef_send.at[step],
+            recv_sem=coef_recv.at[step], device_id={"atom": atom, "energy": other}, device_id_type=MESH,
+        )
+        copy.start()
+        coefs.append(copy)
+    coef_ref[energy] = mine_ref[...]
+
+    keep.wait()
+    for copy in halos:
+        copy.wait_send()
+    for copy in pieces + coefs:
+        copy.wait()
+    rest = q_ref.at[pl.ds(0, devices - 1)]
+    pltpu.make_async_copy(rest, rest, q_send).wait()
+    pltpu.make_async_copy(rest, rest, q_recv).wait()
+    group = LANES // PLANE * energies
+    shift = jnp.zeros((PLANE, 1), f32)
+    for g in range(ring * PLANE // LANES):
+        charges = jnp.sum(q_ref[pl.ds(g * group, group), 0, :], axis=0, keepdims=True)
+        shift = shift + jnp.sum(madelung_ref[:, pl.ds(g * LANES, LANES)] * charges, axis=1, keepdims=True)
+    shift_ref[...] = shift
+
+
+def core_scratch(order, dirs, ring, energies, channels):
     count = max(plan(dirs)[1])
     depth = dirs // 2 * order
+    dma = pltpu.SemaphoreType.DMA
     return [
+        pltpu.VMEM((2, 4, PLANE // 2, order * order), f32),
+        pltpu.VMEM((ring * energies, 1, LANES), f32),
+        pltpu.VMEM((2, PLANE, channels), f32),
+        pltpu.VMEM((order * 16, LANES), f32),
+        pltpu.VMEM((3, order * (PLANE // 2), LANES), f32),
         pltpu.VMEM((8 * order, dirs * 64), bf16),
+        pltpu.VMEM((4 * order, depth), f32),
         pltpu.VMEM((PLANE * order, LANES), bf16),
-        pltpu.VMEM((3, count, PLANE * order, LANES), bf16),
-        pltpu.VMEM((3, count, PLANE * order, LANES), bf16),
+        pltpu.VMEM((3, count, PLANE, order, LANES), bf16),
+        pltpu.VMEM((3, count, PLANE, order, LANES), bf16),
         pltpu.VMEM((depth, PLANE * LANES), bf16),
         pltpu.VMEM((depth, PLANE * LANES), bf16),
         pltpu.VMEM((PLANE // 2 * order, LANES), f32),
+        dma((2,)), dma((2,)), dma((energies,)), dma((energies,)), dma((energies,)), dma((energies,)),
+        dma, dma, dma,
     ]
 
 
 def density_kernel(species_ref, coef_ref, pieces_ref, shift_ref, old_ref, density_ref, potential_ref):
-    kinds, energies = pieces_ref.shape[0], pieces_ref.shape[1]
+    kinds, energies = pieces_ref.shape[1], pieces_ref.shape[0]
     channels, atoms, width = density_ref.shape
     kind = jnp.broadcast_to(species_ref[...], (atoms, width))
     for l in range(channels):
         total = None
         for e in range(energies):
             for z in range(2):
-                row = jnp.broadcast_to(pieces_ref[0, e, 1 - z, l : l + 1, :], (atoms, width))
+                row = jnp.broadcast_to(pieces_ref[e, 0, l, 1 - z : 2 - z, :], (atoms, width))
                 for s in range(1, kinds):
-                    row = jnp.where(kind == s, pieces_ref[s, e, 1 - z, l : l + 1, :], row)
+                    row = jnp.where(kind == s, pieces_ref[e, s, l, 1 - z : 2 - z, :], row)
                 term = coef_ref[e, z, :, l : l + 1] * row
                 total = term if total is None else total + term
         density_ref[l] = total
@@ -208,11 +361,7 @@
 
 VMEM = pl.BlockSpec(memory_space=pltpu.VMEM)
 SMEM = pl.BlockSpec(memory_space=pltpu.SMEM)
-
-
-def neighbour_rings(count):
-    forward = [(i, (i + 1) % count) for i in range(count)]
-    return forward, [(target, source) for source, target in forward]
+MESH = pl.DeviceIdType.MESH
 
 
 def shards(single_site, structure, neighbours, species, valence, energy_weights, gaunt_table,
@@ -225,34 +374,25 @@
     energies = lax.axis_size("energy")
     assert atom_rows == PLANE and energy_rows == 1 and order == 32
 
-    own = single_site.reshape(atom_rows, 2, order, order)
-    own = jnp.transpose(own, (2, 0, 1, 3)).reshape(order, atom_rows * 2 * order)
-    forward, backward = neighbour_rings(lax.axis_size("atom"))
-    low = lax.ppermute(own, "atom", forward)
-    high = lax.ppermute(own, "atom", backward)
-    pieces = lax.all_to_all(radial_shapes, "energy", split_axis=4, concat_axis=1, tiled=True)
-
-    g = structure.reshape(dirs, 2, order, order)
-    g_rows = jnp.transpose(g, (2, 0, 1, 3)).reshape(order, dirs * 2 * order)
-    g2 = g[::-1].reshape(dirs // 2, 2, 2, order, order)
-    g2 = jnp.transpose(g2, (1, 2, 3, 0, 4)).reshape(4 * order, dirs // 2 * order)
-
-    coef = pl.pallas_call(
-        functools.partial(core, order, dirs),
-        out_shape=jax.ShapeDtypeStruct((2, atom_rows, channels), f32),
-        in_specs=[SMEM, SMEM] + [VMEM] * 6,
-        out_specs=VMEM,
-        scratch_shapes=core_scratch(order, dirs),
+    def parts(x):
+        return jnp.transpose(x.reshape(-1, 4, order * order), (1, 0, 2))
+
+    shapes = jnp.transpose(radial_shapes[:, 0], (0, 2, 1, 3))
+    ring = lax.axis_size("atom")
+    coef, pieces, shift = pl.pallas_call(
+        functools.partial(core, order, dirs, ring, energies),
+        out_shape=[
+            jax.ShapeDtypeStruct((energies, 2, atom_rows, channels), f32),
+            jax.ShapeDtypeStruct((energies, kinds, channels, 2, width), f32),
+            jax.ShapeDtypeStruct((atom_rows, 1), f32),
+        ],
+        in_specs=[SMEM] * 3 + [VMEM] * 7,
+        out_specs=[VMEM] * 3,
+        scratch_shapes=core_scratch(order, dirs, ring, energies, channels),
+        compiler_params=pltpu.CompilerParams(collective_id=0, has_side_effects=True),
         name="scatter",
-    )(neighbours % PLANE, energy_weights, low, own, high, g_rows, g2, gaunt_table)
-
-    shape_charge = jnp.sum(radial_shapes[:, 0, :, 0, :] * radial_weights, axis=-1)
-    sums = shape_charge[species]
-    part = coef[0, :, 0] * sums[:, 1] + coef[1, :, 0] * sums[:, 0]
-    local = lax.psum(part, "energy") - valence[species]
-    charges = lax.all_gather(local, "atom", axis=0, tiled=True)
-    shift = jnp.sum(madelung * charges[None, :], axis=1, keepdims=True)
-    coef_all = lax.all_gather(coef, "energy", axis=0)
+    )(neighbours % PLANE, energy_weights, valence, parts(single_site), parts(structure), gaunt_table, shapes,
+      radial_weights[None, :], species[:, None], madelung)
 
     old = jnp.transpose(old_potential, (1, 0, 2))
     density, potential = pl.pallas_call(
@@ -261,7 +401,7 @@
         in_specs=[VMEM] * 5,
         out_specs=[VMEM] * 2,
         name="density",
-    )(species[:, None], coef_all, pieces, shift, old)
+    )(species[:, None], coef, pieces, shift, old)
     back = lambda x: jnp.transpose(x, (1, 0, 2))
     return back(density), back(potential)
 

time: 88 us -> 34.2 us (0.39)
  blocking collectives: 39.1 us -> 0 us
  local copies, waits for them, and re-layouts: 20.8 us -> 4.14 us
  Pallas kernels: 12.9 us -> 28.6 us
  starting transfers between devices: 9.16 us -> 0 us
  other arithmetic: 4.07 us -> 0.6 us
    unnamed x1 -> x0, blocking collectives: 29.5 us -> none
    pallas_call x1, Pallas kernels: 9.89 us -> 25.5 us  [shards(): pl.pallas_call(functools.partial(core, order, dirs, ring, energies), out_...]
    unnamed x29 -> x4, local copies, waits for them, and re-layouts: 8.99 us -> 0.01 us
    ppermute x2 -> x0, starting transfers between devices: 5.56 us -> none  [the longest x1 5.02 us: shards(): high = lax.ppermute(own, 'atom', backward)]
    psum x1 -> x0, blocking collectives: 4.93 us -> none  [shards(): local = lax.psum(part, 'energy') - valence[species]]
    all_gather x1 -> x0, blocking collectives: 4.68 us -> none  [shards(): coef_all = lax.all_gather(coef, 'energy', axis=0)]
    all_to_all x1 -> x0, starting transfers between devices: 3.6 us -> none  [shards(): lax.all_to_all(radial_shapes, 'energy', split_axis=4, concat_axis=1, tile...]
    reshape x7 -> x4, local copies, waits for them, and re-layouts: 5.53 us -> 2.81 us  [parts(): return jnp.transpose(x.reshape(-1, 4, order * order), (1, 0, 2))]
  transfers between devices with their start and end apart: 3 -> 0, of which waited for: 0 -> 0; matrix products, arithmetic and copies ran while one was open for 16% -> 0% of each run, Pallas kernels for 11% -> 0%
where the time goes in v2:
time: 34.2 us; the launch traced here: 34 us
  Pallas kernels  28.6 us (84%)
  local copies, waits for them, and re-layouts  4.14 us (12%)
  between operations  0.66 us (2%)
  other arithmetic  0.6 us (2%)
    pallas_call x1, Pallas kernels, shards(): pl.pallas_call(functools.partial(core, order, dirs, ring, energies), out_...  25.5 us
    pallas_call x1, Pallas kernels, shards(): pl.pallas_call(density_kernel, out_shape=[jax.ShapeDtypeStruct(old.shape,...  3.03 us
    reshape x4, local copies, waits for them, and re-layouts, parts(): return jnp.transpose(x.reshape(-1, 4, order * order), (1, 0, 2))  2.81 us
    broadcast_in_dim x1, local copies, waits for them, and re-layouts, shards(): species[:, None]  1.33 us

profile of v2, /device:TPU:0, one launch (start us, length us, event | category | flops | bytes accessed | tf_op | source)
XLA Modules:
  0.0 34.0 jit_solution(18155690815393154276)
XLA Ops:
  0.6 0.0 copy-start.1
  0.6 1.3 %copy.18.species_ref = s32[16,1]{1,0:T(8,128)} copy(s32[16,1]{0,1:T(1,128)} %bitcast.19) | data formatting | bytes 128 | tf_op jit(solution)/shard_map/broadcast_in_dim | solution.py:404
  2.0 0.0 copy-done.1
  2.0 0.6 %add_select_fusion.nbr_ref = s32[16,26]{1,0:T(8,128)} fusion(s32[16,26]{1,0:T(8,128)S(1)} %copy-done.1), kind=kLoop, calls=%fused_computation.2 | loop fusion | flops 4576 | bytes 3328 | tf_op jit(solution)/shard_map/jit(remainder)/select_n | solution.py:394
  2.6 0.0 copy-start
  2.6 1.1 %reshape.10 = f32[8,4,1024]{2,1,0:T(4,128)S(1)} reshape(f32[16,1,2,1024]{3,2,1,0:T(2,128)} %param.11) | data formatting | bytes 262144 | tf_op jit(solution)/shard_map/reshape | solution.py:378
  3.6 0.7 %copy.22 = f32[8,4,1024]{2,0,1:T(8,128)} copy(f32[8,4,1024]{2,1,0:T(4,128)S(1)} %reshape.10) | data formatting | bytes 262144 | tf_op jit(solution)/shard_map/reshape | solution.py:378
  4.4 0.0 copy-done
  4.4 0.2 reshape.11
  4.6 0.8 %copy.21 = f32[13,4,1024]{2,0,1:T(8,128)} copy(f32[13,4,1024]{2,1,0:T(4,128)S(1)} %reshape.11) | data formatting | bytes 425984 | tf_op jit(solution)/shard_map/reshape | solution.py:378
  5.4 25.5 %scatter.1 = (f32[2,2,16,49]{3,2,1,0:T(8,128)}, f32[2,2,49,2,256]{4,3,2,1,0:T(2,128)}, f32[16,1]{1,0:T(8,128)}) custom-call(s32[16,26]{1,0:T(8,128)} %add_select_fusion.nbr_ref, f32[1,2]{1,0:T(1,128)} %w_ref.1, f32[2]{0:T(128)} %valence_ref.1, f32[4,8,1024]{2,1,0:T(8,128)} %bitcast.16, f32[4,13,1024]{2,1,0:T(8,128)} %bitcast.14, f32[49,1024]{1,0:T(8,128)} %gaunt_ref.1, ...), custom_call_target="tpu_custom_call" | custom-call | tf_op jit(solution)/shard_map/scatter/pallas_call | solution.py:382
  30.9 3.0 %density.1 = (f32[49,16,256]{2,1,0:T(8,128)}, f32[49,16,256]{2,1,0:T(8,128)}) custom-call(s32[16,1]{1,0:T(8,128)} %copy.18.species_ref, f32[2,2,16,49]{3,2,1,0:T(8,128)} %get-tuple-element.7.coef_ref, f32[2,2,49,2,256]{4,3,2,1,0:T(2,128)} %get-tuple-element.8.pieces_ref, f32[16,1]{1,0:T(8,128)} %get-tuple-element.9.shift_ref, f32[49,16,256]{2,1,0:T(8,128)} %bitcast.15), custom_call_target="tpu_custom_call" | custom-call | tf_op jit(solution)/shard_map/density/pallas_call | solution.py:398
Async XLA Ops:
  0.6 1.3 %copy-start.1 = (s32[16,26]{1,0:T(8,128)S(1)}, s32[16,26]{1,0:T(8,128)}, u32[]{:S(2)}) copy-start(s32[16,26]{1,0:T(8,128)} %param.13) | copy-start | bytes 4996
  2.6 1.8 %copy-start = (f32[1,26,2,1024]{3,2,1,0:T(2,128)S(1)}, f32[1,26,2,1024]{3,2,1,0:T(2,128)}, u32[]{:S(2)}) copy-start(f32[1,26,2,1024]{3,2,1,0:T(2,128)} %param.12) | copy-start | bytes 638980

commit v3 on v2

--- a/solution.py
+++ b/solution.py
@@ -71,9 +71,10 @@
                 x = g if shift == 0 else pltpu.roll(g, shift, 1)
                 joined[row] = x if place == 0 else jnp.where(lane == place, x, joined[row])
                 if place == 3 or t == blocks - 1:
-                    g2_ref[pl.ds(row * order, order), pl.ds(t // 4 * LANES, 32 * (place + 1))] = (
-                        joined[row][:, : 32 * (place + 1)]
-                    )
+                    lanes = pl.ds(t // 4 * LANES, 32 * (place + 1))
+                    high, low = split(joined[row][:, : 32 * (place + 1)])
+                    g2_ref[pl.ds(row * order, order), lanes] = high
+                    g2_ref[pl.ds((4 + row) * order, order), lanes] = low
 
 
 def plane_products(x, lhs_ref, rhs_ref, rhigh_ref, rlow_ref, plane, first, count, order):
@@ -103,7 +104,7 @@
         t = b // 2
         half = slice((b % 2) * 64, (b % 2) * 64 + 64)
         for a in range(PLANE):
-            n = nbr_ref[a, k]
+            n = nbr_ref[a, k] & (PLANE - 1)
             to = (pl.ds(t * order, order), pl.ds(a * LANES + (b % 2) * 64, 64))
             yhigh_ref[to] = rhigh_ref[plane, t - first, n][:, half]
             ylow_ref[to] = rlow_ref[plane, t - first, n][:, half]
@@ -134,28 +135,31 @@
     return o[:order, :LANES] + o[order:, :LANES] + o[:order, LANES:]
 
 
-def path_and_project(own, g2_ref, yhigh_ref, ylow_ref, gaunt_ref, v_ref, order):
+def path_and_project(own, g2_ref, yhigh_ref, ylow_ref, wt_ref, gaunt_ref, v_ref, order):
     low_lane, real_lane = tile_masks(order)
     low2, _ = tile_masks(2 * order)
-    gh, gl = split(g2_ref[...])
-    rows = gh.shape[0]
-    both = jnp.concatenate([gh, gl], axis=0)
-    for pair in range(PLANE // 2):
+    both = g2_ref[...]
+    rows = both.shape[0] // 2
+    half = rows // 2
+    gh = both[:rows]
+    pairs = range(PLANE // 2)
+    cs = []
+    for pair in pairs:
         lanes = pl.ds(pair * 2 * LANES, 2 * LANES)
         d = dot(both, yhigh_ref[:, lanes])
         s = d[:rows] + d[rows:] + dot(gh, ylow_ref[:, lanes])
-        half = rows // 2
         e0, o0 = s[:half, :LANES], s[half:, :LANES]
         e1, o1 = s[:half, LANES:], s[half:, LANES:]
         m = jnp.where(low2, e0, o1) + pltpu.roll(jnp.where(low2, e1, o0), 64, 1)
-        c = m[:order] + times_i(m[order:], real_lane)
-        t = own(pair)
-        q = pair_product(c, weights_of(t, low_lane, real_lane), order)
-        wq = weights_of(q, low_lane, real_lane)
-        v = t
-        for _ in range(TERMS - 1):
-            v = t + pair_product(v, wq, order)
-        v_ref[pl.ds(pair * order, order), :] = v
+        cs.append(m[:order] + times_i(m[order:], real_lane))
+    qs = [pair_product(cs[pair], wt_ref[pair], order) for pair in pairs]
+    ws = [weights_of(q, low_lane, real_lane) for q in qs]
+    ts = [own(pair) for pair in pairs]
+    vs = ts
+    for _ in range(TERMS - 1):
+        vs = [ts[pair] + pair_product(vs[pair], ws[pair], order) for pair in pairs]
+    for pair in pairs:
+        v_ref[pl.ds(pair * order, order), :] = vs[pair]
     pairs = PLANE // 2
     lane = lax.broadcasted_iota(jnp.int32, (pairs, LANES), 1) // 32
     columns = []
@@ -171,7 +175,7 @@
         columns.append(jnp.concatenate(pieces, axis=0))
     z = jnp.concatenate(columns, axis=1)
     zh, zl = split(z)
-    gh, gl = split(gaunt_ref[...])
+    gh, gl = gaunt_ref[0], gaunt_ref[1]
     nt = (((1,), (1,)), ((), ()))
     d = lax.dot_general(jnp.concatenate([zh, zl], axis=0), gh, nt, preferred_element_type=f32)
     return d[: 2 * PLANE] + d[2 * PLANE :] + lax.dot_general(zh, gl, nt, preferred_element_type=f32)
@@ -197,9 +201,25 @@
     return firsts, counts
 
 
+def density_of(kind, coef_ref, pieces_ref, density_ref):
+    energies, kinds = pieces_ref.shape[:2]
+    channels, atoms, width = density_ref.shape
+    kind = jnp.broadcast_to(kind, (atoms, width))
+    for l in range(channels):
+        total = None
+        for e in range(energies):
+            for z in range(2):
+                row = jnp.broadcast_to(pieces_ref[e, 0, l, 1 - z : 2 - z, :], (atoms, width))
+                for s in range(1, kinds):
+                    row = jnp.where(kind == s, pieces_ref[e, s, l, 1 - z : 2 - z, :], row)
+                term = coef_ref[e, z, :, l : l + 1] * row
+                total = term if total is None else total + term
+        density_ref[l] = total
+
+
 def core(order, dirs, ring, energies, nbr_ref, w_ref, valence_ref, own_ref, g_ref, gaunt_ref, shapes_ref,
-         weights_ref, species_ref, madelung_ref, coef_ref, pieces_ref, shift_ref,
-         halo_ref, q_ref, mine_ref, wg_ref, wt_ref, rhs_ref, g2_ref, lhs_ref, rhigh_ref, rlow_ref,
+         weights_ref, species_ref, madelung_ref, density_ref, shift_ref,
+         coef_ref, pieces_ref, total_ref, wd_ref, table_ref, halo_ref, q_ref, mine_ref, wg_ref, wt_ref, rhs_ref, g2_ref, lhs_ref, rhigh_ref, rlow_ref,
          yhigh_ref, ylow_ref, v_ref, halo_send, halo_recv, piece_send, piece_recv, coef_send, coef_recv,
          q_send, q_recv, local_sem):
     atom, energy = lax.axis_index("atom"), lax.axis_index("energy")
@@ -220,7 +240,7 @@
     lax.fori_loop(1, devices, greet, 0)
 
     firsts, counts = plan(dirs)
-    to_rows(lambda m, lanes: g_ref[m, :, lanes], dirs // 2, wg_ref, order)
+    to_rows(lambda m, lanes: g_ref[:, m // 2, m % 2, lanes], dirs // 2, wg_ref, order)
     prepare_couplings(wg_ref, rhs_ref, g2_ref, order, dirs // 2)
     pl.semaphore_wait(barrier, devices - 1)
 
@@ -256,9 +276,17 @@
                        index, firsts[index], counts[index], order)
         gather(nbr_ref, rhigh_ref, rlow_ref, yhigh_ref, ylow_ref, dirs, index, firsts[index], order)
 
-    plane(1, lambda m, lanes: own_ref[m, :, lanes])
-
-    kind = species_ref[...]
+    plane(1, lambda m, lanes: own_ref[:, m // 2, m % 2, lanes])
+
+    low_lane, real_lane = tile_masks(order)
+    for pair in range(PLANE // 2):
+        wd_ref[pair] = weights_of(tile_of(wt_ref.at[1], pair, order), low_lane, real_lane)
+    table_ref[0], table_ref[1] = split(gaunt_ref[...])
+
+    row = lax.broadcasted_iota(jnp.int32, (PLANE, PLANE), 0)
+    lane = lax.broadcasted_iota(jnp.int32, (PLANE, PLANE), 1)
+    kinds_row = jnp.broadcast_to(species_ref[...].astype(f32), (PLANE, PLANE))
+    kind = jnp.sum(jnp.where(row == lane, kinds_row, jnp.zeros((PLANE, PLANE), f32)), axis=1, keepdims=True)
     sums = [None, None]
     base = jnp.zeros(kind.shape, f32)
     for s in range(kinds):
@@ -271,10 +299,10 @@
 
     for side, index in ((0, 0), (1, 2)):
         halos[side].wait_recv()
-        plane(index, lambda m, lanes, side=side: halo_ref[side, m, :, lanes])
+        plane(index, lambda m, lanes, side=side: halo_ref[side, :, m // 2, m % 2, lanes])
 
     own = lambda pair: tile_of(wt_ref.at[1], pair, order)
-    projected = path_and_project(own, g2_ref, yhigh_ref, ylow_ref, gaunt_ref, v_ref, order)
+    projected = path_and_project(own, g2_ref, yhigh_ref, ylow_ref, wd_ref, table_ref, v_ref, order)
     store_scaled(projected, w_ref[0, 0], w_ref[0, 1], mine_ref)
 
     q = mine_ref[0, :, 0:1] * sums[0] + mine_ref[1, :, 0:1] * sums[1] - base
@@ -303,10 +331,13 @@
     coef_ref[energy] = mine_ref[...]
 
     keep.wait()
+    for copy in pieces + coefs:
+        copy.wait()
+    density_of(kind, coef_ref, pieces_ref, total_ref)
+    out = pltpu.make_async_copy(total_ref, density_ref, local_sem)
+    out.start()
     for copy in halos:
         copy.wait_send()
-    for copy in pieces + coefs:
-        copy.wait()
     rest = q_ref.at[pl.ds(0, devices - 1)]
     pltpu.make_async_copy(rest, rest, q_send).wait()
     pltpu.make_async_copy(rest, rest, q_recv).wait()
@@ -316,20 +347,26 @@
         charges = jnp.sum(q_ref[pl.ds(g * group, group), 0, :], axis=0, keepdims=True)
         shift = shift + jnp.sum(madelung_ref[:, pl.ds(g * LANES, LANES)] * charges, axis=1, keepdims=True)
     shift_ref[...] = shift
-
-
-def core_scratch(order, dirs, ring, energies, channels):
+    out.wait()
+
+
+def core_scratch(order, dirs, ring, energies, channels, kinds, width):
     count = max(plan(dirs)[1])
     depth = dirs // 2 * order
     dma = pltpu.SemaphoreType.DMA
     return [
-        pltpu.VMEM((2, 4, PLANE // 2, order * order), f32),
+        pltpu.VMEM((energies, 2, PLANE, channels), f32),
+        pltpu.VMEM((energies, kinds, channels, 2, width), f32),
+        pltpu.VMEM((channels, PLANE, width), f32),
+        pltpu.VMEM((PLANE // 2, LANES, 2 * LANES), bf16),
+        pltpu.VMEM((2, channels, order * order), bf16),
+        pltpu.VMEM((2, PLANE // 2, 2, 2, order * order), f32),
         pltpu.VMEM((ring * energies, 1, LANES), f32),
         pltpu.VMEM((2, PLANE, channels), f32),
         pltpu.VMEM((order * 16, LANES), f32),
         pltpu.VMEM((3, order * (PLANE // 2), LANES), f32),
         pltpu.VMEM((8 * order, dirs * 64), bf16),
-        pltpu.VMEM((4 * order, depth), f32),
+        pltpu.VMEM((8 * order, depth), bf16),
         pltpu.VMEM((PLANE * order, LANES), bf16),
         pltpu.VMEM((3, count, PLANE, order, LANES), bf16),
         pltpu.VMEM((3, count, PLANE, order, LANES), bf16),
@@ -341,24 +378,6 @@
     ]
 
 
-def density_kernel(species_ref, coef_ref, pieces_ref, shift_ref, old_ref, density_ref, potential_ref):
-    kinds, energies = pieces_ref.shape[1], pieces_ref.shape[0]
-    channels, atoms, width = density_ref.shape
-    kind = jnp.broadcast_to(species_ref[...], (atoms, width))
-    for l in range(channels):
-        total = None
-        for e in range(energies):
-            for z in range(2):
-                row = jnp.broadcast_to(pieces_ref[e, 0, l, 1 - z : 2 - z, :], (atoms, width))
-                for s in range(1, kinds):
-                    row = jnp.where(kind == s, pieces_ref[e, s, l, 1 - z : 2 - z, :], row)
-                term = coef_ref[e, z, :, l : l + 1] * row
-                total = term if total is None else total + term
-        density_ref[l] = total
-        added = total + shift_ref[...] if l == 0 else total
-        potential_ref[l] = (1.0 - mixing) * old_ref[l] + mixing * added
-
-
 VMEM = pl.BlockSpec(memory_space=pltpu.VMEM)
 SMEM = pl.BlockSpec(memory_space=pltpu.SMEM)
 MESH = pl.DeviceIdType.MESH
@@ -375,33 +394,28 @@
     assert atom_rows == PLANE and energy_rows == 1 and order == 32
 
     def parts(x):
-        return jnp.transpose(x.reshape(-1, 4, order * order), (1, 0, 2))
+        return x.reshape(-1, 2, 2, order * order)
 
     shapes = jnp.transpose(radial_shapes[:, 0], (0, 2, 1, 3))
     ring = lax.axis_size("atom")
-    coef, pieces, shift = pl.pallas_call(
+    density, shift = pl.pallas_call(
         functools.partial(core, order, dirs, ring, energies),
         out_shape=[
-            jax.ShapeDtypeStruct((energies, 2, atom_rows, channels), f32),
-            jax.ShapeDtypeStruct((energies, kinds, channels, 2, width), f32),
+            jax.ShapeDtypeStruct((channels, atom_rows, width), f32),
             jax.ShapeDtypeStruct((atom_rows, 1), f32),
         ],
         in_specs=[SMEM] * 3 + [VMEM] * 7,
-        out_specs=[VMEM] * 3,
-        scratch_shapes=core_scratch(order, dirs, ring, energies, channels),
+        out_specs=[pl.BlockSpec(memory_space=pl.ANY), VMEM],
+        scratch_shapes=core_scratch(order, dirs, ring, energies, channels, kinds, width),
         compiler_params=pltpu.CompilerParams(collective_id=0, has_side_effects=True),
         name="scatter",
-    )(neighbours % PLANE, energy_weights, valence, parts(single_site), parts(structure), gaunt_table, shapes,
-      radial_weights[None, :], species[:, None], madelung)
+    )(neighbours, energy_weights, valence, parts(single_site), parts(structure), gaunt_table, shapes,
+      radial_weights[None, :], species[None, :], madelung)
 
     old = jnp.transpose(old_potential, (1, 0, 2))
-    density, potential = pl.pallas_call(
-        density_kernel,
-        out_shape=[jax.ShapeDtypeStruct(old.shape, f32)] * 2,
-        in_specs=[VMEM] * 5,
-        out_specs=[VMEM] * 2,
-        name="density",
-    )(species[:, None], coef, pieces, shift, old)
+    channel = lax.broadcasted_iota(jnp.int32, (channels, 1, 1), 0)
+    added = jnp.where(channel == 0, shift[None], jnp.float32(0.0))
+    potential = (1.0 - mixing) * old + mixing * (density + added)
     back = lambda x: jnp.transpose(x, (1, 0, 2))
     return back(density), back(potential)
 

time: 34.2 us -> 26.7 us (0.78)
  Pallas kernels: 28.6 us -> 21.7 us
  local copies, waits for them, and re-layouts: 4.14 us -> 0.89 us
  other arithmetic: 0.6 us -> 3.19 us
    pallas_call x1, Pallas kernels: 25.5 us -> 21.7 us  [shards(): pl.pallas_call(functools.partial(core, order, dirs, ring, energies), out_...]
    pallas_call x1 -> x0, Pallas kernels: 3.03 us -> none  [shards(): pl.pallas_call(density_kernel, out_shape=[jax.ShapeDtypeStruct(old.shape,...]
    reshape x4 -> x0, local copies, waits for them, and re-layouts: 2.81 us -> none  [parts(): return jnp.transpose(x.reshape(-1, 4, order * order), (1, 0, 2))]
    transpose x0 -> x1, other arithmetic: none -> 2.3 us  [shards(): back = lambda x: jnp.transpose(x, (1, 0, 2))]
    broadcast_in_dim x1 -> x0, local copies, waits for them, and re-layouts: 1.33 us -> none  [shards(): species[:, None]]
    unnamed x4 -> x5, local copies, waits for them, and re-layouts: 0.01 us -> 0.89 us
    pallas_call x0 -> x1, other arithmetic: none -> 0.81 us  [shards(): pl.pallas_call(functools.partial(core, order, dirs, ring, energies), out_...]
    select_n x1, other arithmetic: 0.6 us -> 0.08 us  [shards(): added = jnp.where(channel == 0, shift[None], jnp.float32(0.0))]
where the time goes in v3:
time: 26.7 us; the launch traced here: 26.5 us
  Pallas kernels  21.7 us (81%)
  other arithmetic  3.19 us (12%)
  local copies, waits for them, and re-layouts  0.89 us (3%)
  between operations  0.67 us (3%)
    pallas_call x1, Pallas kernels, shards(): pl.pallas_call(functools.partial(core, order, dirs, ring, energies), out_...  21.7 us
    transpose x1, other arithmetic, shards(): back = lambda x: jnp.transpose(x, (1, 0, 2))  2.3 us
    unnamed x5, local copies, waits for them, and re-layouts  0.89 us
    pallas_call x1, other arithmetic, shards(): pl.pallas_call(functools.partial(core, order, dirs, ring, energies), out_...  0.81 us

profile of v3, /device:TPU:0, one launch (start us, length us, event | category | flops | bytes accessed | tf_op | source)
XLA Modules:
  0.0 26.5 jit_solution(8515584350894381832)
XLA Ops:
  0.6 0.0 copy-start.1
  0.7 21.7 %scatter.1 = (f32[49,16,256]{2,1,0:T(8,128)}, f32[16,1]{1,0:T(8,128)}) custom-call(s32[16,26]{1,0:T(8,128)} %nbr_ref.1, f32[1,2]{1,0:T(1,128)} %w_ref.1, f32[2]{0:T(128)} %valence_ref.1, f32[8,2,2,1024]{3,2,1,0:T(2,128)} %bitcast.17, f32[13,2,2,1024]{3,2,1,0:T(2,128)} %bitcast.16, f32[49,1024]{1,0:T(8,128)} %gaunt_ref.1, f32[2,49,2,512]{3,2,1,0:T(2,128)} %bitcast.15, ...), custom_call_target="tpu_custom_call" | custom-call | tf_op jit(solution)/shard_map/scatter/pallas_call | solution.py:401
  22.4 0.8 %reduce = f32[16]{0:T(128)S(1)} reduce(f32[16,1]{1,0:T(8,128)} %get-tuple-element.5, f32[]{:T(128)} %constant.12), dimensions={1}, to_apply=%get-tuple-element.5.reduce_sub_computation | reduce | bytes 132 | tf_op jit(solution)/shard_map/scatter/pallas_call | solution.py:401
  23.2 0.1 broadcast_select_fusion
  23.2 0.0 copy-done.1
  23.3 0.0 copy-start
  23.3 2.3 %fusion = f32[16,49,256]{2,0,1:T(8,128)} fusion(f32[49,16,256]{2,1,0:T(8,128)} %get-tuple-element.4, f32[16,49,256]{2,0,1:T(8,128)S(1)} %copy-done.1, f32[49,16]{1,0:T(8,128)S(1)} %broadcast_select_fusion), kind=kLoop, calls=%fused_computation.1 | loop fusion | flops 802816 | bytes 2411584 | tf_op jit(solution)/shard_map/transpose | solution.py:419
  25.6 0.0 copy-done
  25.6 0.9 %copy.14 = f32[16,49,256]{2,0,1:T(8,128)} copy(f32[16,49,256]{2,0,1:T(8,128)S(1)} %bitcast.14) | data formatting | bytes 1605632
  (1 shorter events, 0.0 us)
Async XLA Ops:
  0.6 22.6 %copy-start.1 = (f32[16,49,256]{2,0,1:T(8,128)S(1)}, f32[16,49,256]{2,0,1:T(8,128)}, u32[]{:S(2)}) copy-start(f32[16,49,256]{2,0,1:T(8,128)} %param.21) | copy-start | bytes 2408452
  23.3 2.3 %copy-start = (f32[49,16,256]{2,1,0:T(8,128)S(1)}, f32[49,16,256]{2,1,0:T(8,128)}, u32[]{:S(2)}) copy-start(f32[49,16,256]{2,1,0:T(8,128)} %get-tuple-element.4) | copy-start | bytes 2408452

commit v4 on v3

--- a/solution.py
+++ b/solution.py
@@ -201,7 +201,7 @@
     return firsts, counts
 
 
-def density_of(kind, coef_ref, pieces_ref, density_ref):
+def density_of(kind, coef_ref, pieces_ref, old_ref, density_ref, mixed_ref):
     energies, kinds = pieces_ref.shape[:2]
     channels, atoms, width = density_ref.shape
     kind = jnp.broadcast_to(kind, (atoms, width))
@@ -215,13 +215,15 @@
                 term = coef_ref[e, z, :, l : l + 1] * row
                 total = term if total is None else total + term
         density_ref[l] = total
+        if l > 0:
+            mixed_ref[l - 1] = (1.0 - mixing) * old_ref[l] + mixing * total
 
 
 def core(order, dirs, ring, energies, nbr_ref, w_ref, valence_ref, own_ref, g_ref, gaunt_ref, shapes_ref,
-         weights_ref, species_ref, madelung_ref, density_ref, shift_ref,
-         coef_ref, pieces_ref, total_ref, wd_ref, table_ref, halo_ref, q_ref, mine_ref, wg_ref, wt_ref, rhs_ref, g2_ref, lhs_ref, rhigh_ref, rlow_ref,
+         weights_ref, species_ref, madelung_ref, previous_ref, density_ref, potential_ref,
+         coef_ref, pieces_ref, total_ref, old_ref, mixed_ref, first_ref, wd_ref, table_ref, halo_ref, q_ref, mine_ref, wg_ref, wt_ref, rhs_ref, g2_ref, lhs_ref, rhigh_ref, rlow_ref,
          yhigh_ref, ylow_ref, v_ref, halo_send, halo_recv, piece_send, piece_recv, coef_send, coef_recv,
-         q_send, q_recv, local_sem):
+         q_send, q_recv, local_sem, old_sem, mixed_sem, first_sem):
     atom, energy = lax.axis_index("atom"), lax.axis_index("energy")
     devices = ring * energies
     me = atom * energies + energy
@@ -231,6 +233,8 @@
         other = lax.rem(me + step, devices)
         return {"atom": other // energies, "energy": lax.rem(other, energies)}
 
+    fetch = pltpu.make_async_copy(previous_ref, old_ref, old_sem)
+    fetch.start()
     barrier = pltpu.get_barrier_semaphore()
 
     def greet(step, carry):
@@ -333,9 +337,12 @@
     keep.wait()
     for copy in pieces + coefs:
         copy.wait()
-    density_of(kind, coef_ref, pieces_ref, total_ref)
+    fetch.wait()
+    density_of(kind, coef_ref, pieces_ref, old_ref, total_ref, mixed_ref)
     out = pltpu.make_async_copy(total_ref, density_ref, local_sem)
     out.start()
+    upper = pltpu.make_async_copy(mixed_ref, potential_ref.at[pl.ds(1, mixed_ref.shape[0])], mixed_sem)
+    upper.start()
     for copy in halos:
         copy.wait_send()
     rest = q_ref.at[pl.ds(0, devices - 1)]
@@ -346,8 +353,12 @@
     for g in range(ring * PLANE // LANES):
         charges = jnp.sum(q_ref[pl.ds(g * group, group), 0, :], axis=0, keepdims=True)
         shift = shift + jnp.sum(madelung_ref[:, pl.ds(g * LANES, LANES)] * charges, axis=1, keepdims=True)
-    shift_ref[...] = shift
+    first_ref[0] = (1.0 - mixing) * old_ref[0] + mixing * (total_ref[0] + shift)
+    last = pltpu.make_async_copy(first_ref, potential_ref.at[pl.ds(0, 1)], first_sem)
+    last.start()
     out.wait()
+    upper.wait()
+    last.wait()
 
 
 def core_scratch(order, dirs, ring, energies, channels, kinds, width):
@@ -358,6 +369,9 @@
         pltpu.VMEM((energies, 2, PLANE, channels), f32),
         pltpu.VMEM((energies, kinds, channels, 2, width), f32),
         pltpu.VMEM((channels, PLANE, width), f32),
+        pltpu.VMEM((channels, PLANE, width), f32),
+        pltpu.VMEM((channels - 1, PLANE, width), f32),
+        pltpu.VMEM((1, PLANE, width), f32),
         pltpu.VMEM((PLANE // 2, LANES, 2 * LANES), bf16),
         pltpu.VMEM((2, channels, order * order), bf16),
         pltpu.VMEM((2, PLANE // 2, 2, 2, order * order), f32),
@@ -374,12 +388,13 @@
         pltpu.VMEM((depth, PLANE * LANES), bf16),
         pltpu.VMEM((PLANE // 2 * order, LANES), f32),
         dma((2,)), dma((2,)), dma((energies,)), dma((energies,)), dma((energies,)), dma((energies,)),
-        dma, dma, dma,
+        dma, dma, dma, dma, dma, dma,
     ]
 
 
 VMEM = pl.BlockSpec(memory_space=pltpu.VMEM)
 SMEM = pl.BlockSpec(memory_space=pltpu.SMEM)
+ANY = pl.BlockSpec(memory_space=pl.ANY)
 MESH = pl.DeviceIdType.MESH
 
 
@@ -398,24 +413,18 @@
 
     shapes = jnp.transpose(radial_shapes[:, 0], (0, 2, 1, 3))
     ring = lax.axis_size("atom")
-    density, shift = pl.pallas_call(
+    density, potential = pl.pallas_call(
         functools.partial(core, order, dirs, ring, energies),
-        out_shape=[
-            jax.ShapeDtypeStruct((channels, atom_rows, width), f32),
-            jax.ShapeDtypeStruct((atom_rows, 1), f32),
-        ],
-        in_specs=[SMEM] * 3 + [VMEM] * 7,
-        out_specs=[pl.BlockSpec(memory_space=pl.ANY), VMEM],
+        out_shape=[jax.ShapeDtypeStruct((channels, atom_rows, width), f32)] * 2,
+        in_specs=[SMEM] * 3 + [VMEM] * 7 + [ANY],
+        out_specs=[ANY] * 2,
         scratch_shapes=core_scratch(order, dirs, ring, energies, channels, kinds, width),
         compiler_params=pltpu.CompilerParams(collective_id=0, has_side_effects=True),
         name="scatter",
     )(neighbours, energy_weights, valence, parts(single_site), parts(structure), gaunt_table, shapes,
-      radial_weights[None, :], species[None, :], madelung)
-
-    old = jnp.transpose(old_potential, (1, 0, 2))
-    channel = lax.broadcasted_iota(jnp.int32, (channels, 1, 1), 0)
-    added = jnp.where(channel == 0, shift[None], jnp.float32(0.0))
-    potential = (1.0 - mixing) * old + mixing * (density + added)
+      radial_weights[None, :], species[None, :], madelung,
+      jnp.transpose(old_potential, (1, 0, 2)))
+
     back = lambda x: jnp.transpose(x, (1, 0, 2))
     return back(density), back(potential)
 

time: 26.7 us -> 25.5 us (0.955)
  other arithmetic: 3.19 us -> 0 us
  local copies, waits for them, and re-layouts: 0.89 us -> 3.04 us
    transpose x1 -> x0, other arithmetic: 2.3 us -> none  [shards(): back = lambda x: jnp.transpose(x, (1, 0, 2))]
    unnamed x5 -> x4, local copies, waits for them, and re-layouts: 0.89 us -> 3.04 us
    pallas_call x1 -> x0, other arithmetic: 0.81 us -> none  [shards(): pl.pallas_call(functools.partial(core, order, dirs, ring, energies), out_...]
where the time goes in v4:
time: 25.5 us; the launch traced here: 25.3 us
  Pallas kernels  21.7 us (85%)
  local copies, waits for them, and re-layouts  3.04 us (12%)
  between operations  0.65 us (3%)
    pallas_call x1, Pallas kernels, shards(): pl.pallas_call(functools.partial(core, order, dirs, ring, energies), out_...  21.7 us
    unnamed x4, local copies, waits for them, and re-layouts  3.04 us

profile of v4, /device:TPU:0, one launch (start us, length us, event | category | flops | bytes accessed | tf_op | source)
XLA Modules:
  0.0 25.3 jit_solution(8954109702901056186)
XLA Ops:
  0.6 21.7 %scatter.1 = (f32[49,16,256]{2,1,0:T(8,128)}, f32[49,16,256]{2,1,0:T(8,128)}) custom-call(s32[16,26]{1,0:T(8,128)} %nbr_ref.1, f32[1,2]{1,0:T(1,128)} %w_ref.1, f32[2]{0:T(128)} %valence_ref.1, f32[8,2,2,1024]{3,2,1,0:T(2,128)} %bitcast.15, f32[13,2,2,1024]{3,2,1,0:T(2,128)} %bitcast.14, f32[49,1024]{1,0:T(8,128)} %gaunt_ref.1, f32[2,49,2,512]{3,2,1,0:T(2,128)} %bitcast.13, ...), custom_call_target="tpu_custom_call" | custom-call | tf_op jit(solution)/shard_map/scatter/pallas_call | solution.py:416
  22.3 0.0 copy-start
  22.3 2.2 %copy.15 = f32[16,49,256]{2,0,1:T(8,128)} copy(f32[16,49,256]{2,0,1:T(8,128)} %bitcast.12) | data formatting | bytes 1605632
  24.5 0.0 copy-done
  24.5 0.9 %copy.16 = f32[16,49,256]{2,0,1:T(8,128)} copy(f32[16,49,256]{2,0,1:T(8,128)S(1)} %bitcast.11) | data formatting | bytes 1605632
Async XLA Ops:
  22.3 2.2 %copy-start = (f32[49,16,256]{2,1,0:T(8,128)S(1)}, f32[49,16,256]{2,1,0:T(8,128)}, u32[]{:S(2)}) copy-start(f32[49,16,256]{2,1,0:T(8,128)} %get-tuple-element.5) | copy-start | bytes 2408452
